TPU v7x, 512 devices: a whole 4x8x8 slice. The times are simulated.
512 devices in a mesh: tok: 64 (over z_hi, x, y), tp: 8 (over z_lo, core).
Axes of the slice: x: 4, y: 8, z: 8 (z_hi: 2, z_lo: 4; z = z_hi * 4 + z_lo), core: 2. Of those that a mesh axis runs over, the one named last changes fastest.
Arguments:
- tokens: bfloat16 [8192, 4096], P('tok', 'tp'), may hold values from -6 to 6
- w_query: bfloat16 [4096, 4096], P('tok', 'tp'), may hold values from -0.09375 to 0.09375
- w_key: bfloat16 [4096, 4096], P('tok', 'tp'), may hold values from -0.09375 to 0.09375
- w_value: bfloat16 [4096, 4096], P('tok', 'tp'), may hold values from -0.09375 to 0.09375
- short_taps: float32 [3, 3, 4096], P(None, None, 'tp'), may hold values from -3.5 to 3.5
- filters: float32 [4096, 8192], P(('tp', 'tok')), may hold values from -90 to 90, as said below
- skip_gain: float32 [4096], P(('tp', 'tok')), may hold values from 0.1 to 1.9
Outputs:
- layer_out: bfloat16 [8192, 4096], P('tok', 'tp')
Inputs may be any that keep to these rules, and one draw needn't show every extreme that they name: `filters`: real-valued filter taps.
All inputs are finite; a program needn't handle non-finite values.
Results may differ from a plain program's by a relative error of at most 0.009.
Values may be sent and summed in bfloat16 or wider, within the bound.
No kernel may reach another device: no remote copies, remote signals or barrier semaphores. Data moves between devices by JAX's collectives and lax.ppermute only.
A program may use at most 64 MiB of HBM per device.

v0:
```python
import math

import jax
import jax.numpy as jnp
import numpy as np
from jax import lax
from jax.experimental import pallas as pl
from jax.experimental.pallas import tpu as pltpu
from jax.sharding import Mesh
from jax.sharding import PartitionSpec as P

AXES = ("z_hi", "x", "yh", "yl", "z_lo", "core")
SIZES = (2, 4, 4, 2, 4, 2)
TOK = AXES[:4]
TP = AXES[4:]
HALO = 8
BLOCK = 128
ROWS = HALO + BLOCK
POINTS = 128
F32 = jnp.float32
BF16 = jnp.bfloat16


def exchanged(value, axes):
    return lax.all_to_all(value, axes, split_axis=0, concat_axis=0, tiled=True)


def from_everyone(value, axes, apart=()):
    count = math.prod(SIZES[AXES.index(a)] for a in axes)
    copies = jnp.broadcast_to(value, (count, *value.shape))
    if apart:
        copies = copies.reshape(-1, *value.shape[1:])
    return exchanged(copies, axes + apart)


def dft_tables():
    n = np.arange(POINTS)
    full = 2.0 * np.pi * (np.outer(n, n) % POINTS) / POINTS
    cos, sin = np.cos(full), np.sin(full)
    half = POINTS // 2
    outer = np.concatenate([cos, -sin], axis=0)
    outer = np.concatenate([outer, outer], axis=1)
    inner = np.block([[cos, -sin], [sin, cos]])
    back_inner = np.block([[cos, sin], [-sin, cos]])
    back_outer = np.concatenate([cos[:half], -sin[:half]], axis=1) / POINTS**2
    twist = 2.0 * np.pi * np.outer(n, n) / POINTS**2
    tables = np.concatenate([inner, back_inner, outer, back_outer], axis=0)
    turns = np.concatenate([np.cos(twist), np.sin(twist)], axis=0)
    return jnp.asarray(tables, F32).astype(BF16), jnp.asarray(turns, F32)


def dot(a, b):
    return jnp.dot(a, b, preferred_element_type=F32)


def spectrum(rows, tables, turns):
    cos, sin = turns[0:POINTS], turns[POINTS:]
    blocks = jnp.concatenate(
        [rows[pl.ds(c, 64, stride=8), :].astype(BF16) for c in range(8)], axis=1
    )
    first = dot(tables[512:768, 0:64], blocks)
    turned = []
    for c in range(8):
        re = first[:POINTS, c * POINTS : (c + 1) * POINTS]
        im = first[POINTS:, c * POINTS : (c + 1) * POINTS]
        turned.append(
            jnp.concatenate([re * cos + im * sin, im * cos - re * sin], axis=1).astype(BF16)
        )
    return dot(jnp.concatenate(turned, axis=0), tables[0:256])


def filter_kernel(filters, tables, turns, spec, tables_out, turns_out, rows):
    tables_out[...] = tables[...]
    turns_out[...] = turns[...]
    taps = filters[...]
    unit = taps / jnp.sqrt(jnp.sum(taps * taps, axis=1, keepdims=True) + 1e-06)
    for b in range(64):
        rows[pl.ds(b * 8, 8), :] = unit[:, b * POINTS : (b + 1) * POINTS]
    spec[...] = spectrum(rows, tables, turns)


def conv_kernel(signal, spec, skip, tables, turns, mixed, rows, out):
    for z in range(2):
        rows[pl.ds(z * 256, 256), :] = signal[:, z].astype(F32).reshape(256, POINTS)
    cos, sin = turns[0:POINTS], turns[POINTS:]
    sig = spectrum(rows, tables, turns)
    re, im = sig[:, :POINTS], sig[:, POINTS:]
    f_re, f_im = spec[:, :POINTS], spec[:, POINTS:]
    prod = jnp.concatenate([re * f_re - im * f_im, re * f_im + im * f_re], axis=1)
    back = dot(prod.astype(BF16), tables[256:512])
    turned = []
    for c in range(8):
        b_re = back[c * POINTS : (c + 1) * POINTS, :POINTS]
        b_im = back[c * POINTS : (c + 1) * POINTS, POINTS:]
        turned.append(
            jnp.concatenate([b_re * cos - b_im * sin, b_re * sin + b_im * cos], axis=0).astype(BF16)
        )
    result = dot(tables[768:832], jnp.concatenate(turned, axis=1))
    for c in range(8):
        piece = result[:, c * POINTS : (c + 1) * POINTS]
        out[pl.ds(c, 64, stride=8), :] = piece + skip[c] * rows[pl.ds(c, 64, stride=8), :]
    for z in range(2):
        mixed[:, z] = out[pl.ds(z * 256, 256), :].astype(BF16).reshape(16, 2, 8, POINTS)


def order_table(rows_are_natural):
    shape = (512, 512)
    row = lax.broadcasted_iota(jnp.int32, shape, 0)
    col = lax.broadcasted_iota(jnp.int32, shape, 1)
    grouped, natural = (col, row) if rows_are_natural else (row, col)
    quarter, xy, j = grouped // 128, (grouped // 8) % 16, grouped % 8
    place = (quarter // 2) * 256 + xy * 16 + (quarter % 2) * 8 + j
    return (natural == place).astype(F32).astype(BF16)


def weights_kernel(where, w_key, w_value, w_query, mine, theirs, held, sems):
    copies = fetched((w_key, w_value, w_query), [held.at[p] for p in range(3)], sems)
    table = order_table(True)
    lower = where[2] < 2
    for p in range(3):
        copies[p].wait()
        cols = dot(held[p], table)
        ours = jnp.where(lower, cols[:, :256], cols[:, 256:]).astype(BF16)
        others = jnp.where(lower, cols[:, 256:], cols[:, :256]).astype(BF16)
        for yl in range(2):
            mine[yl, p] = ours[:, yl * 128 : (yl + 1) * 128]
            theirs[yl, p] = others[:, yl * 128 : (yl + 1) * 128]


def fetched(sources, held, sems):
    copies = [pltpu.make_async_copy(a, b, sems.at[i]) for i, (a, b) in enumerate(zip(sources, held))]
    for copy in copies:
        copy.start()
    return copies


def projected(where, features, w, acc, ready):
    for i, (half, low) in enumerate((h, l) for h in range(2) for l in (0, 2, 1, 3)):
        if i % 2 == 0:
            for copy in ready(i // 2):
                copy.wait()
        pieces = [
            features[half * 4 + parity * 2 + low % 2][(low // 2) * 2 : (low // 2) * 2 + 2]
            for parity in range(2)
        ]
        rows = jnp.concatenate([p.reshape(2 * ROWS, 512) for p in pieces], axis=0)
        term = dot(rows, w(i // 2, part_of(where, half, low)))
        if i == 0:
            acc[...] = term
        else:
            acc[...] += term


def part_of(where, half, low):
    return ((where[0] ^ low) & 3) * 2 + (where[1] ^ half)


def group_of(where, i):
    return ((i % 2) * 2 + i // 2) ^ where[2]


def short(acc, group, at, taps):
    top = group * ROWS + HALO
    cols = pl.ds(at, 128)
    return (
        taps[0:1] * acc[pl.ds(top, BLOCK), cols]
        + taps[1:2] * acc[pl.ds(top - 1, BLOCK), cols]
        + taps[2:3] * acc[pl.ds(top - 2, BLOCK), cols]
    )


def key_value_kernel(where, *refs):
    sources, (taps, out), (w, *held), (acc, sems) = refs[:9], refs[9:11], refs[11:20], refs[20:]
    pairs = [(half, low) for half in range(2) for low in range(2)]
    columns = [sources[0].at[part_of(where, half, low) & 3] for half, low in pairs]
    order = [half * 4 + parity * 2 + low for half, low in pairs for parity in range(2)]
    froms, targets = [], []
    for j in range(4):
        froms += [columns[j], sources[1 + order[2 * j]], sources[1 + order[2 * j + 1]]]
        targets += [w.at[j], held[order[2 * j]], held[order[2 * j + 1]]]
    copies = fetched(froms, targets, sems)

    def weights(j, part):
        z_hi = (part >> 2) ^ where[3]
        return jnp.concatenate([w[j, :, p, z_hi].reshape(512, 128) for p in range(2)], axis=1)

    projected(where, held, weights, acc, lambda j: copies[3 * j : 3 * j + 3])
    for i in range(4):
        keyed = short(acc, i, 0, taps[1])
        valued = short(acc, i, 128, taps[2])
        out[:, group_of(where, i)] = (keyed * valued).T.reshape(16, 8, BLOCK).astype(BF16)


def query_kernel(where, *refs):
    sources, (taps, out), (w, *held), (acc, sems) = refs[:12], refs[12:14], refs[14:23], refs[23:]
    copies = fetched(sources, [w.at[d] for d in range(4)] + held, sems)

    def weights(j, part):
        return w[(part & 3) ^ where[4], :, (part >> 2) ^ where[3]].reshape(512, 128)

    projected(where, held, weights, acc, lambda j: copies if j == 0 else [])
    for i in range(4):
        out[group_of(where, i)] = short(acc, i, 0, taps[0]).astype(BF16)


def gate_kernel(query, returned, out):
    for group in range(4):
        mixed = returned[:, group].astype(F32).reshape(128, BLOCK).T
        out[group] = (query[group].astype(F32) * mixed).astype(BF16)


def order_kernel(gated, out):
    cols = jnp.concatenate([gated[g] for g in range(4)], axis=1)
    out[...] = dot(cols, order_table(False)).astype(BF16)


def call(kernel, out_shape, args, scratch=(), in_specs=None, flops=10**8):
    whole = pl.BlockSpec(memory_space=pltpu.VMEM)
    specs = in_specs or [whole] * len(args)
    moved = sum(math.prod(a.shape) * a.dtype.itemsize for a in args)
    return pl.pallas_call(
        kernel,
        out_shape=out_shape,
        in_specs=specs,
        out_specs=jax.tree.map(lambda _: whole, out_shape),
        scratch_shapes=list(scratch),
        compiler_params=pltpu.CompilerParams(vmem_limit_bytes=20 * 2**20),
        cost_estimate=pl.CostEstimate(flops=flops, bytes_accessed=moved, transcendentals=0),
    )(*args)


def of_previous(value, axes):
    count = math.prod(SIZES[AXES.index(a)] for a in axes)
    return lax.ppermute(value, axes, [(i, i + 1) for i in range(count - 1)])


def swapped(value, axes, bits):
    count = math.prod(SIZES[AXES.index(a)] for a in axes)
    return lax.ppermute(value, axes, [(i, i ^ bits) for i in range(count)])


def mixer(tokens, w_query, w_key, w_value, short_taps, filters, skip_gain):
    shape = jax.ShapeDtypeStruct
    whole = pl.BlockSpec(memory_space=pltpu.VMEM)
    smem = pl.BlockSpec(memory_space=pltpu.SMEM)
    place = lax.axis_index(AXES)
    core, z_lo, yl, x, z_hi = place % 2, place // 2 % 4, place // 8 % 2, place // 64 % 4, place // 256
    where = jnp.stack([z_hi * 4 + z_lo, core, z_hi * 2 + yl, z_hi, x])

    anywhere = pl.BlockSpec(memory_space=pl.ANY)
    halo = of_previous(tokens[-HALO:], TOK)
    part = shape((2, 3, 64, 128), BF16)
    own, others = call(
        weights_kernel,
        (part, part),
        (where, *(pltpu.with_memory_space_constraint(w, pltpu.HBM) for w in (w_key, w_value, w_query))),
        (pltpu.VMEM((3, 64, 512), BF16), pltpu.SemaphoreType.DMA((3,))),
        in_specs=[smem] + [anywhere] * 3,
    )
    got = swapped(others, ("z_hi",), 1)
    first = from_everyone(jnp.stack([own, got], axis=2), ("yh",), ("yl",))

    ring = ("z_hi", "z_lo")
    mine = jnp.concatenate([halo, tokens], axis=0)[None]
    far_block = swapped(mine, ring, 4)
    two = jnp.concatenate([mine, far_block], axis=0)
    even = jnp.concatenate([two, swapped(two, ring, 2)], axis=0)
    taps = short_taps.reshape(3, 3, 2, 16, 2, 8)
    taps = lax.dynamic_index_in_dim(taps, z_hi, 2, keepdims=False)
    taps = lax.dynamic_index_in_dim(taps, yl, 3, keepdims=False).reshape(3, 3, 128)

    first, taps, where, _ = lax.optimization_barrier((first, taps, where, even))
    weights = from_everyone(first[:, :2], ("x",))
    odd = swapped(even, ring, 1)
    even_y = swapped(even, ("yl",), 1)
    odd_y = swapped(odd, ("yl",), 1)
    ours = (even, odd, even_y, odd_y)
    features = list(ours)
    for blocks in ours:
        features.append(swapped(blocks, ("core",), 1))
    slice_of_first, last = lax.optimization_barrier((first[:, 2], features[-1]))
    features = (*features[:-1], last)
    query_weights = [slice_of_first]
    query_weights += [swapped(query_weights[0], ("x",), d) for d in (1, 2, 3)]

    kept = [pltpu.with_memory_space_constraint(v, pltpu.HBM) for v in features]
    blocks = [pltpu.VMEM((4, ROWS, 512), BF16)] * 8
    key_value = call(
        key_value_kernel,
        shape((16, 4, 8, BLOCK), BF16),
        (where, weights, *kept, taps),
        [pltpu.VMEM((4, 8, 2, 2, 64, 128), BF16)]
        + blocks
        + [pltpu.VMEM((4 * ROWS, 256), F32), pltpu.SemaphoreType.DMA((12,))],
        in_specs=[smem] + [anywhere] * 9 + [whole],
        flops=2 * 544 * 4096 * 256,
    )
    owned = exchanged(key_value, ("x", "yh"))
    tables, turns = dft_tables()
    filters, _ = lax.optimization_barrier((filters, key_value))
    spec, tables, turns = call(
        filter_kernel,
        (shape((8 * POINTS, 2 * POINTS), F32), shape(tables.shape, BF16), shape(turns.shape, F32)),
        (filters, tables, turns),
        (pltpu.VMEM((512, POINTS), F32),),
    )
    owned, spec = lax.optimization_barrier((owned, spec))
    mixed = call(
        conv_kernel,
        shape((16, 2, 2, 8, BLOCK), BF16),
        (owned.reshape(16, 2, 2, 8, BLOCK), spec, skip_gain, tables, turns),
        (pltpu.VMEM((512, POINTS), F32), pltpu.VMEM((512, POINTS), F32)),
        in_specs=[whole, whole, smem, whole, whole],
        flops=2 * 168 * 10**6,
    )
    returned = exchanged(mixed.reshape(16, 4, 8, BLOCK), ("x", "yh"))
    taps, _ = lax.optimization_barrier((taps, mixed))
    query = call(
        query_kernel,
        shape((4, BLOCK, 128), BF16),
        (where, *query_weights, *kept, taps),
        [pltpu.VMEM((4, 8, 2, 64, 128), BF16)]
        + blocks
        + [pltpu.VMEM((4 * ROWS, 128), F32), pltpu.SemaphoreType.DMA((12,))],
        in_specs=[smem] + [anywhere] * 12 + [whole],
        flops=2 * 544 * 4096 * 128,
    )
    gated = call(gate_kernel, shape((4, BLOCK, 128), BF16), (query, returned))
    gated = exchanged(gated, ("z_hi", "yl"))
    return call(order_kernel, shape((BLOCK, 512), BF16), (gated,))


def solution(mesh):
    fine = Mesh(mesh.devices.reshape(SIZES), AXES)
    in_specs = (
        P(TOK, TP),
        P(TOK, TP),
        P(TOK, TP),
        P(TOK, TP),
        P(None, None, TP),
        P(TP + TOK, None),
        P(TP + TOK),
    )
    return jax.shard_map(mixer, mesh=fine, in_specs=in_specs, out_specs=P(TOK, TP), check_vma=False)
```

profile of v0, /device:TPU:6, one launch (start us, length us, event | category | flops | bytes accessed | tf_op | source)
XLA Modules:
  0.0 182.8 jit_solution(12359554767069444054)
XLA Ops:
  2.1 10.9 %collective-permute-start = (bf16[2,3,64,128]{3,2,1,0:T(8,128)(2,1)S(1)}, bf16[2,3,64,128]{3,2,1,0:T(8,128)(2,1)S(1)}, u32[]{:S(2)}, u32[]{:S(2)}) collective-permute-start(bf16[2,3,64,128]{3,2,1,0:T(8,128)(2,1)S(1)} %get-tuple-element.20), channel_id=1, source_target_pairs={{0,256},{256,0},{1,257},{257,1},{2,258},{258,2},{3,259},{259,3},{4... | collective-permute-start | bytes 294920 | tf_op jit(solution)/shard_map/ppermute | solution.py:239
  13.0 2.9 %collective-permute-done = bf16[2,3,64,128]{3,2,1,0:T(8,128)(2,1)S(1)} collective-permute-done((bf16[2,3,64,128]{3,2,1,0:T(8,128)(2,1)S(1)}, bf16[2,3,64,128]{3,2,1,0:T(8,128)(2,1)S(1)}, u32[]{:S(2)}, u32[]{:S(2)}) %collective-permute-start) | collective-permute-done | bytes 98336 | tf_op jit(solution)/shard_map/ppermute | solution.py:239
  17.0 7.1 %all-to-all-start = ((bf16[8,3,2,64,128]{4,3,2,1,0:T(8,128)(2,1)}), bf16[8,3,2,64,128]{4,3,2,1,0:T(8,128)(2,1)S(1)}, u32[]{:S(2)}, u32[]{:S(2)}) async-start(bf16[8,3,2,64,128]{4,3,2,1,0:T(8,128)(2,1)} %bitcast.7), calls=%async_computation | async-start | bytes 1572864 | tf_op jit(solution)/shard_map/all_to_all | solution.py:25
  24.2 3.9 %collective-permute-start.1 = (bf16[8,512]{1,0:T(8,128)(2,1)S(1)}, bf16[8,512]{1,0:T(8,128)(2,1)S(1)}, u32[]{:S(2)}, u32[]{:S(2)}) collective-permute-start(bf16[8,512]{1,0:T(8,128)(2,1)S(1)} %slice.9), channel_id=1, source_target_pairs={{0,8},{8,16},{16,24},{24,32},{32,40},{40,48},{48,56},{56,64},{64,7... | collective-permute-start | bytes 24584 | tf_op jit(solution)/shard_map/ppermute | solution.py:234
  28.1 12.4 %collective-permute-done.1 = bf16[8,512]{1,0:T(8,128)(2,1)S(1)} collective-permute-done((bf16[8,512]{1,0:T(8,128)(2,1)S(1)}, bf16[8,512]{1,0:T(8,128)(2,1)S(1)}, u32[]{:S(2)}, u32[]{:S(2)}) %collective-permute-start.1) | collective-permute-done | bytes 8224 | tf_op jit(solution)/shard_map/ppermute | solution.py:234
  40.6 8.2 %collective-permute-start.2 = (bf16[1,136,512]{2,1,0:T(8,128)(2,1)S(1)}, bf16[1,136,512]{2,1,0:T(8,128)(2,1)S(1)}, u32[]{:S(2)}, u32[]{:S(2)}) collective-permute-start(bf16[1,136,512]{2,1,0:T(8,128)(2,1)S(1)} %maximum_bitcast_fusion), channel_id=1, source_target_pairs={{0,256},{2,258},{4,260},{6,262},{256,0},{258,2},{260,4},{262,6},{1... | collective-permute-start | bytes 417800 | tf_op jit(solution)/shard_map/ppermute | solution.py:239
  48.7 5.5 %collective-permute-done.2 = bf16[1,136,512]{2,1,0:T(8,128)(2,1)S(1)} collective-permute-done((bf16[1,136,512]{2,1,0:T(8,128)(2,1)S(1)}, bf16[1,136,512]{2,1,0:T(8,128)(2,1)S(1)}, u32[]{:S(2)}, u32[]{:S(2)}) %collective-permute-start.2) | collective-permute-done | bytes 139296 | tf_op jit(solution)/shard_map/ppermute | solution.py:239
  54.3 4.9 %collective-permute-start.3 = (bf16[2,136,512]{2,1,0:T(8,128)(2,1)S(1)}, bf16[2,136,512]{2,1,0:T(8,128)(2,1)S(1)}, u32[]{:S(2)}, u32[]{:S(2)}) collective-permute-start(bf16[2,136,512]{2,1,0:T(8,128)(2,1)S(1)} %pad_maximum_fusion.1), channel_id=1, source_target_pairs={{0,4},{2,6},{4,0},{6,2},{256,260},{258,262},{260,256},{262,258},{1... | collective-permute-start | bytes 835592 | tf_op jit(solution)/shard_map/ppermute | solution.py:239
  59.1 9.9 %collective-permute-done.3 = bf16[2,136,512]{2,1,0:T(8,128)(2,1)S(1)} collective-permute-done((bf16[2,136,512]{2,1,0:T(8,128)(2,1)S(1)}, bf16[2,136,512]{2,1,0:T(8,128)(2,1)S(1)}, u32[]{:S(2)}, u32[]{:S(2)}) %collective-permute-start.3) | collective-permute-done | bytes 278560 | tf_op jit(solution)/shard_map/ppermute | solution.py:239
  74.6 4.5 %all-to-all-start.1 = ((bf16[4,8,2,2,64,128]{5,4,3,2,1,0:T(8,128)(2,1)}), bf16[4,8,2,2,64,128]{5,4,3,2,1,0:T(8,128)(2,1)S(1)}, u32[]{:S(2)}, u32[]{:S(2)}) async-start(bf16[4,8,2,2,64,128]{5,4,3,2,1,0:T(8,128)(2,1)} %broadcast_in_dim.11), calls=%async_computation.1 | async-start | bytes 4194304 | tf_op jit(solution)/shard_map/all_to_all | solution.py:25
  79.1 7.0 %collective-permute-done.4.refs_2_.refs_5_ = bf16[4,136,512]{2,1,0:T(8,128)(2,1)} collective-permute-done((bf16[4,136,512]{2,1,0:T(8,128)(2,1)}, bf16[4,136,512]{2,1,0:T(8,128)(2,1)}, u32[]{:S(2)}, u32[]{:S(2)}) %collective-permute-start.4) | collective-permute-done | bytes 557088 | tf_op jit(solution)/shard_map/ppermute | solution.py:239
  88.0 3.9 %collective-permute-start.10 = (bf16[4,136,512]{2,1,0:T(8,128)(2,1)}, bf16[4,136,512]{2,1,0:T(8,128)(2,1)S(1)}, u32[]{:S(2)}, u32[]{:S(2)}) collective-permute-start(bf16[4,136,512]{2,1,0:T(8,128)(2,1)} %pad_maximum_fusion.refs_1_.refs_4_), channel_id=1, source_target_pairs={{0,8},{8,0},{1,9},{9,1},{2,10},{10,2},{3,11},{11,3},{4,12},{12,4},... | collective-permute-start | bytes 1671176 | tf_op jit(solution)/shard_map/ppermute | solution.py:239
  91.9 11.7 %collective-permute-done.5.refs_4_.refs_7_ = bf16[4,136,512]{2,1,0:T(8,128)(2,1)S(1)} collective-permute-done((bf16[4,136,512]{2,1,0:T(8,128)(2,1)}, bf16[4,136,512]{2,1,0:T(8,128)(2,1)S(1)}, u32[]{:S(2)}, u32[]{:S(2)}) %collective-permute-start.5) | collective-permute-done | bytes 557088 | tf_op jit(solution)/shard_map/ppermute | solution.py:239
  105.6 2.4 %collective-permute-start.11 = (bf16[4,136,512]{2,1,0:T(8,128)(2,1)}, bf16[4,136,512]{2,1,0:T(8,128)(2,1)S(1)}, u32[]{:S(2)}, u32[]{:S(2)}) collective-permute-start(bf16[4,136,512]{2,1,0:T(8,128)(2,1)} %pad_maximum_fusion.refs_1_.refs_4_), channel_id=1, source_target_pairs={{0,1},{1,0},{2,3},{3,2},{4,5},{5,4},{6,7},{7,6},{8,9},{9,8},{10,11... | collective-permute-start | bytes 1671176 | tf_op jit(solution)/shard_map/ppermute | solution.py:239
  109.9 3.3 %collective-permute-done.10.refs_3_.refs_6_ = bf16[4,136,512]{2,1,0:T(8,128)(2,1)S(1)} collective-permute-done((bf16[4,136,512]{2,1,0:T(8,128)(2,1)}, bf16[4,136,512]{2,1,0:T(8,128)(2,1)S(1)}, u32[]{:S(2)}, u32[]{:S(2)}) %collective-permute-start.10) | collective-permute-done | bytes 557088 | tf_op jit(solution)/shard_map/ppermute | solution.py:239
  117.2 5.4 %shard_map.92 = bf16[16,4,8,128]{3,2,1,0:T(8,128)(2,1)} custom-call(s32[5]{0:T(128)S(1)} %stack.32.where, bf16[4,8,2,2,64,128]{5,4,3,2,1,0:T(8,128)(2,1)S(1)} %all-to-all-done.1.refs_0_, bf16[4,136,512]{2,1,0:T(8,128)(2,1)} %pad_maximum_fusion.refs_1_.refs_4_, bf16[4,136,512]{2,1,0:T(8,128)(2,1)} %collective-permute-done.4.refs_2_.refs_5_, ...), custom_call_target="tpu_custom_call" | custom-call | flops 1140850688 | bytes 6558228 | tf_op jit(solution)/shard_map/pallas_call | solution.py:221
  122.6 13.2 %all-to-all-start.2 = ((bf16[16,4,8,128]{3,2,1,0:T(8,128)(2,1)}), bf16[16,4,8,128]{3,2,1,0:T(8,128)(2,1)S(1)}, u32[]{:S(2)}, u32[]{:S(2)}) async-start(bf16[16,4,8,128]{3,2,1,0:T(8,128)(2,1)} %shard_map.92), calls=%async_computation.2 | async-start | bytes 262144 | tf_op jit(solution)/shard_map/all_to_all | solution.py:25
  135.9 2.8 %collective-permute-start.7 = (bf16[8,2,64,128]{3,2,1,0:T(8,128)(2,1)S(1)}, bf16[8,2,64,128]{3,2,1,0:T(8,128)(2,1)S(1)}, u32[]{:S(2)}, u32[]{:S(2)}) collective-permute-start(bf16[8,2,64,128]{3,2,1,0:T(8,128)(2,1)S(1)} %slice_bitcast_fusion.refs_0_), channel_id=1, source_target_pairs={{0,64},{64,0},{128,192},{192,128},{1,65},{65,1},{129,193},{193,129... | collective-permute-start | bytes 786440 | tf_op jit(solution)/shard_map/ppermute | solution.py:239
  138.6 2.6 %collective-permute-start.8 = (bf16[8,2,64,128]{3,2,1,0:T(8,128)(2,1)S(1)}, bf16[8,2,64,128]{3,2,1,0:T(8,128)(2,1)S(1)}, u32[]{:S(2)}, u32[]{:S(2)}) collective-permute-start(bf16[8,2,64,128]{3,2,1,0:T(8,128)(2,1)S(1)} %slice_bitcast_fusion.refs_0_), channel_id=1, source_target_pairs={{0,128},{64,192},{128,0},{192,64},{1,129},{65,193},{129,1},{193,65... | collective-permute-start | bytes 786440 | tf_op jit(solution)/shard_map/ppermute | solution.py:239
  141.3 5.0 %collective-permute-start.9 = (bf16[8,2,64,128]{3,2,1,0:T(8,128)(2,1)S(1)}, bf16[8,2,64,128]{3,2,1,0:T(8,128)(2,1)}, u32[]{:S(2)}, u32[]{:S(2)}) collective-permute-start(bf16[8,2,64,128]{3,2,1,0:T(8,128)(2,1)S(1)} %slice_bitcast_fusion.refs_0_), channel_id=1, source_target_pairs={{0,192},{64,128},{128,64},{192,0},{1,193},{65,129},{129,65},{193,1... | collective-permute-start | bytes 786440 | tf_op jit(solution)/shard_map/ppermute | solution.py:239
  149.2 9.3 %all-to-all-start.3 = ((bf16[16,4,8,128]{3,2,1,0:T(8,128)(2,1)}), bf16[16,4,8,128]{3,2,1,0:T(8,128)(2,1)S(1)}, u32[]{:S(2)}, u32[]{:S(2)}) async-start(bf16[16,4,8,128]{3,2,1,0:T(8,128)(2,1)} %bitcast.11), calls=%async_computation.3 | async-start | bytes 262144 | tf_op jit(solution)/shard_map/all_to_all | solution.py:25
  158.6 4.4 %shard_map.95.query = bf16[4,128,128]{2,1,0:T(8,128)(2,1)S(1)} custom-call(s32[5]{0:T(128)S(1)} %stack.32.where, bf16[8,2,64,128]{3,2,1,0:T(8,128)(2,1)S(1)} %slice_bitcast_fusion.refs_0_, bf16[8,2,64,128]{3,2,1,0:T(8,128)(2,1)S(1)} %collective-permute-done.7.refs_1_, bf16[8,2,64,128]{3,2,1,0:T(8,128)(2,1)S(1)} %collective-permute-done.8.refs_2_, ...), custom_call_target="tpu_custom_call" | custom-call | flops 570425344 | bytes 5509652 | tf_op jit(solution)/shard_map/pallas_call | solution.py:221
  163.0 4.0 %all-to-all-done.3.returned = bf16[16,4,8,128]{3,2,1,0:T(8,128)(2,1)S(1)} async-done(((bf16[16,4,8,128]{3,2,1,0:T(8,128)(2,1)}), bf16[16,4,8,128]{3,2,1,0:T(8,128)(2,1)S(1)}, u32[]{:S(2)}, u32[]{:S(2)}) %all-to-all-start.3) | async-done | bytes 131104 | tf_op jit(solution)/shard_map/all_to_all | solution.py:25
  167.1 14.7 %all_to_all.25.gated = bf16[4,128,128]{2,1,0:T(8,128)(2,1)S(1)} all-to-all(bf16[4,128,128]{2,1,0:T(8,128)(2,1)S(1)} %shard_map.96), channel_id=1, replica_groups=mesh['z_hi'=2,'x'=4,'yh'=4,'yl'=2,'z_lo'=4,'core'=2] {'z_hi','yl'}, dimensions={0} | all-to-all | bytes 262144 | tf_op jit(solution)/shard_map/all_to_all | solution.py:25
  (56 shorter events, 22.3 us)
Async XLA Ops:
  0.0 24.2 %copy-start.9 = (bf16[128,512]{1,0:T(8,128)(2,1)S(1)}, bf16[128,512]{1,0:T(8,128)(2,1)}, u32[]{:S(2)}) copy-start(bf16[128,512]{1,0:T(8,128)(2,1)} %param.9) | copy-start | bytes 393220
  2.1 13.8 %collective-permute-start = (bf16[2,3,64,128]{3,2,1,0:T(8,128)(2,1)S(1)}, bf16[2,3,64,128]{3,2,1,0:T(8,128)(2,1)S(1)}, u32[]{:S(2)}, u32[]{:S(2)}) collective-permute-start(bf16[2,3,64,128]{3,2,1,0:T(8,128)(2,1)S(1)} %get-tuple-element.20), channel_id=1, source_target_pairs={{0,256},{256,0},{1,257},{257,1},{2,258},{258,2},{3,259},{259,3},{4... | collective-permute-start | bytes 294920 | tf_op jit(solution)/shard_map/ppermute | solution.py:239
  16.0 55.8 %copy-start.10 = (f32[3,3,512]{2,1,0:T(4,128)S(1)}, f32[3,3,512]{2,1,0:T(4,128)}, u32[]{:S(2)}) copy-start(f32[3,3,512]{2,1,0:T(4,128)} %param.13) | copy-start | bytes 55300
  17.0 55.6 %all-to-all-start = ((bf16[8,3,2,64,128]{4,3,2,1,0:T(8,128)(2,1)}), bf16[8,3,2,64,128]{4,3,2,1,0:T(8,128)(2,1)S(1)}, u32[]{:S(2)}, u32[]{:S(2)}) async-start(bf16[8,3,2,64,128]{4,3,2,1,0:T(8,128)(2,1)} %bitcast.7), calls=%async_computation | async-start | bytes 1572864 | tf_op jit(solution)/shard_map/all_to_all | solution.py:25
  24.2 16.4 %collective-permute-start.1 = (bf16[8,512]{1,0:T(8,128)(2,1)S(1)}, bf16[8,512]{1,0:T(8,128)(2,1)S(1)}, u32[]{:S(2)}, u32[]{:S(2)}) collective-permute-start(bf16[8,512]{1,0:T(8,128)(2,1)S(1)} %slice.9), channel_id=1, source_target_pairs={{0,8},{8,16},{16,24},{24,32},{32,40},{40,48},{48,56},{56,64},{64,7... | collective-permute-start | bytes 24584 | tf_op jit(solution)/shard_map/ppermute | solution.py:234
  40.6 13.7 %collective-permute-start.2 = (bf16[1,136,512]{2,1,0:T(8,128)(2,1)S(1)}, bf16[1,136,512]{2,1,0:T(8,128)(2,1)S(1)}, u32[]{:S(2)}, u32[]{:S(2)}) collective-permute-start(bf16[1,136,512]{2,1,0:T(8,128)(2,1)S(1)} %maximum_bitcast_fusion), channel_id=1, source_target_pairs={{0,256},{2,258},{4,260},{6,262},{256,0},{258,2},{260,4},{262,6},{1... | collective-permute-start | bytes 417800 | tf_op jit(solution)/shard_map/ppermute | solution.py:239
  54.3 14.7 %collective-permute-start.3 = (bf16[2,136,512]{2,1,0:T(8,128)(2,1)S(1)}, bf16[2,136,512]{2,1,0:T(8,128)(2,1)S(1)}, u32[]{:S(2)}, u32[]{:S(2)}) collective-permute-start(bf16[2,136,512]{2,1,0:T(8,128)(2,1)S(1)} %pad_maximum_fusion.1), channel_id=1, source_target_pairs={{0,4},{2,6},{4,0},{6,2},{256,260},{258,262},{260,256},{262,258},{1... | collective-permute-start | bytes 835592 | tf_op jit(solution)/shard_map/ppermute | solution.py:239
  69.9 16.2 %collective-permute-start.4 = (bf16[4,136,512]{2,1,0:T(8,128)(2,1)}, bf16[4,136,512]{2,1,0:T(8,128)(2,1)}, u32[]{:S(2)}, u32[]{:S(2)}) collective-permute-start(bf16[4,136,512]{2,1,0:T(8,128)(2,1)} %pad_maximum_fusion.refs_1_.refs_4_), channel_id=1, source_target_pairs={{0,2},{2,0},{4,6},{6,4},{256,258},{258,256},{260,262},{262,260},{1... | collective-permute-start | bytes 1671176 | tf_op jit(solution)/shard_map/ppermute | solution.py:239
  74.6 42.7 %all-to-all-start.1 = ((bf16[4,8,2,2,64,128]{5,4,3,2,1,0:T(8,128)(2,1)}), bf16[4,8,2,2,64,128]{5,4,3,2,1,0:T(8,128)(2,1)S(1)}, u32[]{:S(2)}, u32[]{:S(2)}) async-start(bf16[4,8,2,2,64,128]{5,4,3,2,1,0:T(8,128)(2,1)} %broadcast_in_dim.11), calls=%async_computation.1 | async-start | bytes 4194304 | tf_op jit(solution)/shard_map/all_to_all | solution.py:25
  86.1 17.6 %collective-permute-start.5 = (bf16[4,136,512]{2,1,0:T(8,128)(2,1)}, bf16[4,136,512]{2,1,0:T(8,128)(2,1)S(1)}, u32[]{:S(2)}, u32[]{:S(2)}) collective-permute-start(bf16[4,136,512]{2,1,0:T(8,128)(2,1)} %collective-permute-done.4.refs_2_.refs_5_), channel_id=1, source_target_pairs={{0,8},{8,0},{1,9},{9,1},{2,10},{10,2},{3,11},{11,3},{4,12},{12,4},... | collective-permute-start | bytes 1671176 | tf_op jit(solution)/shard_map/ppermute | solution.py:239
  88.0 25.3 %collective-permute-start.10 = (bf16[4,136,512]{2,1,0:T(8,128)(2,1)}, bf16[4,136,512]{2,1,0:T(8,128)(2,1)S(1)}, u32[]{:S(2)}, u32[]{:S(2)}) collective-permute-start(bf16[4,136,512]{2,1,0:T(8,128)(2,1)} %pad_maximum_fusion.refs_1_.refs_4_), channel_id=1, source_target_pairs={{0,8},{8,0},{1,9},{9,1},{2,10},{10,2},{3,11},{11,3},{4,12},{12,4},... | collective-permute-start | bytes 1671176 | tf_op jit(solution)/shard_map/ppermute | solution.py:239
  103.7 11.6 %collective-permute-start.6 = (bf16[4,136,512]{2,1,0:T(8,128)(2,1)S(1)}, bf16[4,136,512]{2,1,0:T(8,128)(2,1)S(1)}, u32[]{:S(2)}, u32[]{:S(2)}) collective-permute-start(bf16[4,136,512]{2,1,0:T(8,128)(2,1)S(1)} %collective-permute-done.5.refs_4_.refs_7_), channel_id=1, source_target_pairs={{0,1},{1,0},{2,3},{3,2},{4,5},{5,4},{6,7},{7,6},{8,9},{9,8},{10,11... | collective-permute-start | bytes 1671176 | tf_op jit(solution)/shard_map/ppermute | solution.py:239
  105.6 9.7 %collective-permute-start.11 = (bf16[4,136,512]{2,1,0:T(8,128)(2,1)}, bf16[4,136,512]{2,1,0:T(8,128)(2,1)S(1)}, u32[]{:S(2)}, u32[]{:S(2)}) collective-permute-start(bf16[4,136,512]{2,1,0:T(8,128)(2,1)} %pad_maximum_fusion.refs_1_.refs_4_), channel_id=1, source_target_pairs={{0,1},{1,0},{2,3},{3,2},{4,5},{5,4},{6,7},{7,6},{8,9},{9,8},{10,11... | collective-permute-start | bytes 1671176 | tf_op jit(solution)/shard_map/ppermute | solution.py:239
  108.0 7.3 %collective-permute-start.12 = (bf16[4,136,512]{2,1,0:T(8,128)(2,1)}, bf16[4,136,512]{2,1,0:T(8,128)(2,1)S(1)}, u32[]{:S(2)}, u32[]{:S(2)}) collective-permute-start(bf16[4,136,512]{2,1,0:T(8,128)(2,1)} %collective-permute-done.4.refs_2_.refs_5_), channel_id=1, source_target_pairs={{0,1},{1,0},{2,3},{3,2},{4,5},{5,4},{6,7},{7,6},{8,9},{9,8},{10,11... | collective-permute-start | bytes 1671176 | tf_op jit(solution)/shard_map/ppermute | solution.py:239
  113.3 4.0 %collective-permute-start.13 = (bf16[4,136,512]{2,1,0:T(8,128)(2,1)S(1)}, bf16[4,136,512]{2,1,0:T(8,128)(2,1)}, u32[]{:S(2)}, u32[]{:S(2)}) collective-permute-start(bf16[4,136,512]{2,1,0:T(8,128)(2,1)S(1)} %collective-permute-done.10.refs_3_.refs_6_), channel_id=1, source_target_pairs={{0,1},{1,0},{2,3},{3,2},{4,5},{5,4},{6,7},{7,6},{8,9},{9,8},{10,11... | collective-permute-start | bytes 1671176 | tf_op jit(solution)/shard_map/ppermute | solution.py:239
  115.2 31.1 %copy-start = (bf16[832,256]{1,0:T(8,128)(2,1)S(1)}, bf16[832,256]{1,0:T(8,128)(2,1)}, u32[]{:S(2)}) copy-start(bf16[832,256]{1,0:T(8,128)(2,1)} %constant.145.tables) | copy-start | bytes 1277956
  115.2 31.1 %copy-start.1 = (f32[8,8192]{1,0:T(8,128)S(1)}, f32[8,8192]{1,0:T(8,128)}, u32[]{:S(2)}) copy-start(f32[8,8192]{1,0:T(8,128)} %filters) | copy-start | bytes 786436
  115.2 31.1 %copy-start.2 = (f32[256,128]{1,0:T(8,128)S(1)}, f32[256,128]{1,0:T(8,128)}, u32[]{:S(2)}) copy-start(f32[256,128]{1,0:T(8,128)} %constant.142.clone.turns) | copy-start | bytes 393220
  115.2 31.9 %copy-start.3 = (f32[8]{0:T(128)S(1)}, f32[8]{0:T(128)}, u32[]{:S(2)}) copy-start(f32[8]{0:T(128)} %skip.1) | copy-start | bytes 100
  122.6 24.5 %all-to-all-start.2 = ((bf16[16,4,8,128]{3,2,1,0:T(8,128)(2,1)}), bf16[16,4,8,128]{3,2,1,0:T(8,128)(2,1)S(1)}, u32[]{:S(2)}, u32[]{:S(2)}) async-start(bf16[16,4,8,128]{3,2,1,0:T(8,128)(2,1)} %shard_map.92), calls=%async_computation.2 | async-start | bytes 262144 | tf_op jit(solution)/shard_map/all_to_all | solution.py:25
  135.9 22.7 %collective-permute-start.7 = (bf16[8,2,64,128]{3,2,1,0:T(8,128)(2,1)S(1)}, bf16[8,2,64,128]{3,2,1,0:T(8,128)(2,1)S(1)}, u32[]{:S(2)}, u32[]{:S(2)}) collective-permute-start(bf16[8,2,64,128]{3,2,1,0:T(8,128)(2,1)S(1)} %slice_bitcast_fusion.refs_0_), channel_id=1, source_target_pairs={{0,64},{64,0},{128,192},{192,128},{1,65},{65,1},{129,193},{193,129... | collective-permute-start | bytes 786440 | tf_op jit(solution)/shard_map/ppermute | solution.py:239
  138.6 19.9 %collective-permute-start.8 = (bf16[8,2,64,128]{3,2,1,0:T(8,128)(2,1)S(1)}, bf16[8,2,64,128]{3,2,1,0:T(8,128)(2,1)S(1)}, u32[]{:S(2)}, u32[]{:S(2)}) collective-permute-start(bf16[8,2,64,128]{3,2,1,0:T(8,128)(2,1)S(1)} %slice_bitcast_fusion.refs_0_), channel_id=1, source_target_pairs={{0,128},{64,192},{128,0},{192,64},{1,129},{65,193},{129,1},{193,65... | collective-permute-start | bytes 786440 | tf_op jit(solution)/shard_map/ppermute | solution.py:239
  141.3 17.3 %collective-permute-start.9 = (bf16[8,2,64,128]{3,2,1,0:T(8,128)(2,1)S(1)}, bf16[8,2,64,128]{3,2,1,0:T(8,128)(2,1)}, u32[]{:S(2)}, u32[]{:S(2)}) collective-permute-start(bf16[8,2,64,128]{3,2,1,0:T(8,128)(2,1)S(1)} %slice_bitcast_fusion.refs_0_), channel_id=1, source_target_pairs={{0,192},{64,128},{128,64},{192,0},{1,193},{65,129},{129,65},{193,1... | collective-permute-start | bytes 786440 | tf_op jit(solution)/shard_map/ppermute | solution.py:239
  149.2 17.8 %all-to-all-start.3 = ((bf16[16,4,8,128]{3,2,1,0:T(8,128)(2,1)}), bf16[16,4,8,128]{3,2,1,0:T(8,128)(2,1)S(1)}, u32[]{:S(2)}, u32[]{:S(2)}) async-start(bf16[16,4,8,128]{3,2,1,0:T(8,128)(2,1)} %bitcast.11), calls=%async_computation.3 | async-start | bytes 262144 | tf_op jit(solution)/shard_map/all_to_all | solution.py:25
  (5 other events, 16.4 us)
where the time goes:
time: 185 us; the launch traced here: 183 us
  starting transfers between devices  88.3 us (48%)
  waiting for transfers between devices  56.9 us (31%)
  Pallas kernels  15.7 us (8%)
  blocking collectives  14.7 us (8%)
  local copies, waits for them, and re-layouts  5.78 us (3%)
    ppermute x13, starting transfers between devices, swapped(): return lax.ppermute(value, axes, [(i, i ^ bits) for i in range(count)])  50.2 us
    ppermute x13, waiting for transfers between devices, swapped(): return lax.ppermute(value, axes, [(i, i ^ bits) for i in range(count)])  40.5 us
    all_to_all x4, starting transfers between devices, exchanged(): return lax.all_to_all(value, axes, split_axis=0, concat_axis=0, tiled=True)  34.2 us
    pallas_call x7, Pallas kernels, call(): pl.pallas_call(kernel, out_shape=out_shape, in_specs=specs, out_specs=jax...  15.7 us
    all_to_all x1, blocking collectives, exchanged(): return lax.all_to_all(value, axes, split_axis=0, concat_axis=0, tiled=True)  14.7 us
    ppermute x1, waiting for transfers between devices, of_previous(): return lax.ppermute(value, axes, [(i, i + 1) for i in range(count - 1)])  12.4 us
    all_to_all x4, waiting for transfers between devices, exchanged(): return lax.all_to_all(value, axes, split_axis=0, concat_axis=0, tiled=True)  4.04 us
    ppermute x1, starting transfers between devices, of_previous(): return lax.ppermute(value, axes, [(i, i + 1) for i in range(count - 1)])  3.91 us
  transfers between devices with their start and end apart: 18, of which 9 were waited for; matrix products, arithmetic and copies ran while one was open for 2% of the time, Pallas kernels for 4%

commit v1 on v0

--- a/solution.py
+++ b/solution.py
@@ -136,13 +136,10 @@
 
 def projected(where, features, w, acc, ready):
     for i, (half, low) in enumerate((h, l) for h in range(2) for l in (0, 2, 1, 3)):
-        if i % 2 == 0:
-            for copy in ready(i // 2):
-                copy.wait()
-        pieces = [
-            features[half * 4 + parity * 2 + low % 2][(low // 2) * 2 : (low // 2) * 2 + 2]
-            for parity in range(2)
-        ]
+        for copy in ready(i):
+            copy.wait()
+        kind = (low % 2) * 2 + low // 2
+        pieces = [features[half * 8 + parity * 4 + kind][...] for parity in range(2)]
         rows = jnp.concatenate([p.reshape(2 * ROWS, 512) for p in pieces], axis=0)
         term = dot(rows, w(i // 2, part_of(where, half, low)))
         if i == 0:
@@ -170,21 +167,27 @@
 
 
 def key_value_kernel(where, *refs):
-    sources, (taps, out), (w, *held), (acc, sems) = refs[:9], refs[9:11], refs[11:20], refs[20:]
+    sources, (taps, out), (w, *held), (acc, sems) = refs[:17], refs[17:19], refs[19:36], refs[36:]
     pairs = [(half, low) for half in range(2) for low in range(2)]
     columns = [sources[0].at[part_of(where, half, low) & 3] for half, low in pairs]
-    order = [half * 4 + parity * 2 + low for half, low in pairs for parity in range(2)]
-    froms, targets = [], []
-    for j in range(4):
-        froms += [columns[j], sources[1 + order[2 * j]], sources[1 + order[2 * j + 1]]]
-        targets += [w.at[j], held[order[2 * j]], held[order[2 * j + 1]]]
+    froms, targets, needs = [], [], []
+    for j, (half, low) in enumerate(pairs):
+        for kind in (2 * low, 2 * low + 1):
+            begin = len(froms)
+            if kind % 2 == 0:
+                froms.append(columns[j])
+                targets.append(w.at[j])
+            wanted = [half * 8 + parity * 4 + kind for parity in range(2)]
+            froms += [sources[1 + k] for k in wanted]
+            targets += [held[k] for k in wanted]
+            needs.append(slice(begin, len(froms)))
     copies = fetched(froms, targets, sems)
 
     def weights(j, part):
         z_hi = (part >> 2) ^ where[3]
         return jnp.concatenate([w[j, :, p, z_hi].reshape(512, 128) for p in range(2)], axis=1)
 
-    projected(where, held, weights, acc, lambda j: copies[3 * j : 3 * j + 3])
+    projected(where, held, weights, acc, lambda i: copies[needs[i]])
     for i in range(4):
         keyed = short(acc, i, 0, taps[1])
         valued = short(acc, i, 128, taps[2])
@@ -192,13 +195,13 @@
 
 
 def query_kernel(where, *refs):
-    sources, (taps, out), (w, *held), (acc, sems) = refs[:12], refs[12:14], refs[14:23], refs[23:]
+    sources, (taps, out), (w, *held), (acc, sems) = refs[:20], refs[20:22], refs[22:39], refs[39:]
     copies = fetched(sources, [w.at[d] for d in range(4)] + held, sems)
 
     def weights(j, part):
         return w[(part & 3) ^ where[4], :, (part >> 2) ^ where[3]].reshape(512, 128)
 
-    projected(where, held, weights, acc, lambda j: copies if j == 0 else [])
+    projected(where, held, weights, acc, lambda i: copies if i == 0 else [])
     for i in range(4):
         out[group_of(where, i)] = short(acc, i, 0, taps[0]).astype(BF16)
 
@@ -264,35 +267,36 @@
     mine = jnp.concatenate([halo, tokens], axis=0)[None]
     far_block = swapped(mine, ring, 4)
     two = jnp.concatenate([mine, far_block], axis=0)
-    even = jnp.concatenate([two, swapped(two, ring, 2)], axis=0)
+    next_two = swapped(two, ring, 2)
     taps = short_taps.reshape(3, 3, 2, 16, 2, 8)
     taps = lax.dynamic_index_in_dim(taps, z_hi, 2, keepdims=False)
     taps = lax.dynamic_index_in_dim(taps, yl, 3, keepdims=False).reshape(3, 3, 128)
 
-    first, taps, where, _ = lax.optimization_barrier((first, taps, where, even))
+    first, taps, where = lax.optimization_barrier((first, taps, where))
     weights = from_everyone(first[:, :2], ("x",))
-    odd = swapped(even, ring, 1)
-    even_y = swapped(even, ("yl",), 1)
-    odd_y = swapped(odd, ("yl",), 1)
-    ours = (even, odd, even_y, odd_y)
+    ours = [two, next_two]
+    for _ in range(2):
+        ours.append(swapped(ours[len(ours) - 2], ring, 1))
     features = list(ours)
-    for blocks in ours:
-        features.append(swapped(blocks, ("core",), 1))
+    for pair in ours:
+        features.append(swapped(pair, ("yl",), 1))
+    for pair in tuple(features):
+        features.append(swapped(pair, ("core",), 1))
     slice_of_first, last = lax.optimization_barrier((first[:, 2], features[-1]))
     features = (*features[:-1], last)
     query_weights = [slice_of_first]
     query_weights += [swapped(query_weights[0], ("x",), d) for d in (1, 2, 3)]
 
     kept = [pltpu.with_memory_space_constraint(v, pltpu.HBM) for v in features]
-    blocks = [pltpu.VMEM((4, ROWS, 512), BF16)] * 8
+    blocks = [pltpu.VMEM((2, ROWS, 512), BF16)] * 16
     key_value = call(
         key_value_kernel,
         shape((16, 4, 8, BLOCK), BF16),
         (where, weights, *kept, taps),
         [pltpu.VMEM((4, 8, 2, 2, 64, 128), BF16)]
         + blocks
-        + [pltpu.VMEM((4 * ROWS, 256), F32), pltpu.SemaphoreType.DMA((12,))],
-        in_specs=[smem] + [anywhere] * 9 + [whole],
+        + [pltpu.VMEM((4 * ROWS, 256), F32), pltpu.SemaphoreType.DMA((20,))],
+        in_specs=[smem] + [anywhere] * 17 + [whole],
         flops=2 * 544 * 4096 * 256,
     )
     owned = exchanged(key_value, ("x", "yh"))
@@ -321,8 +325,8 @@
         (where, *query_weights, *kept, taps),
         [pltpu.VMEM((4, 8, 2, 64, 128), BF16)]
         + blocks
-        + [pltpu.VMEM((4 * ROWS, 128), F32), pltpu.SemaphoreType.DMA((12,))],
-        in_specs=[smem] + [anywhere] * 12 + [whole],
+        + [pltpu.VMEM((4 * ROWS, 128), F32), pltpu.SemaphoreType.DMA((20,))],
+        in_specs=[smem] + [anywhere] * 20 + [whole],
         flops=2 * 544 * 4096 * 128,
     )
     gated = call(gate_kernel, shape((4, BLOCK, 128), BF16), (query, returned))

time: 185 us -> 179 us (0.968)
  waiting for transfers between devices: 56.9 us -> 34.2 us
  starting transfers between devices: 88.3 us -> 106 us
    ppermute x13 -> x20, waiting for transfers between devices: 40.5 us -> 17.7 us  [swapped(): return lax.ppermute(value, axes, [(i, i ^ bits) for i in range(count)])]
    ppermute x13 -> x20, starting transfers between devices: 50.2 us -> 68.9 us  [swapped(): return lax.ppermute(value, axes, [(i, i ^ bits) for i in range(count)])]
  transfers between devices with their start and end apart: 18 -> 25, of which waited for: 9 -> 6; matrix products, arithmetic and copies ran while one was open for 2% -> 2% of each run, Pallas kernels for 4% -> 4%
where the time goes in v1:
time: 179 us; the launch traced here: 177 us
  starting transfers between devices  106 us (59%)
  waiting for transfers between devices  34.2 us (19%)
  Pallas kernels  15.8 us (9%)
  blocking collectives  13.3 us (7%)
  local copies, waits for them, and re-layouts  6.21 us (3%)
    ppermute x20, starting transfers between devices, swapped(): return lax.ppermute(value, axes, [(i, i ^ bits) for i in range(count)])  68.9 us
    all_to_all x4, starting transfers between devices, exchanged(): return lax.all_to_all(value, axes, split_axis=0, concat_axis=0, tiled=True)  32.9 us
    ppermute x20, waiting for transfers between devices, swapped(): return lax.ppermute(value, axes, [(i, i ^ bits) for i in range(count)])  17.7 us
    pallas_call x7, Pallas kernels, call(): pl.pallas_call(kernel, out_shape=out_shape, in_specs=specs, out_specs=jax...  15.8 us
    all_to_all x1, blocking collectives, exchanged(): return lax.all_to_all(value, axes, split_axis=0, concat_axis=0, tiled=True)  13.3 us
    ppermute x1, waiting for transfers between devices, of_previous(): return lax.ppermute(value, axes, [(i, i + 1) for i in range(count - 1)])  12.5 us
    all_to_all x4, waiting for transfers between devices, exchanged(): return lax.all_to_all(value, axes, split_axis=0, concat_axis=0, tiled=True)  4.06 us
    ppermute x1, starting transfers between devices, of_previous(): return lax.ppermute(value, axes, [(i, i + 1) for i in range(count - 1)])  3.91 us
  transfers between devices with their start and end apart: 25, of which 6 were waited for; matrix products, arithmetic and copies ran while one was open for 2% of the time, Pallas kernels for 4%

profile of v1, /device:TPU:6, one launch (start us, length us, event | category | flops | bytes accessed | tf_op | source)
XLA Modules:
  0.0 176.9 jit_solution(7650929016355688975)
XLA Ops:
  2.1 10.9 %collective-permute-start = (bf16[2,3,64,128]{3,2,1,0:T(8,128)(2,1)S(1)}, bf16[2,3,64,128]{3,2,1,0:T(8,128)(2,1)S(1)}, u32[]{:S(2)}, u32[]{:S(2)}) collective-permute-start(bf16[2,3,64,128]{3,2,1,0:T(8,128)(2,1)S(1)} %get-tuple-element.20), channel_id=1, source_target_pairs={{0,256},{256,0},{1,257},{257,1},{2,258},{258,2},{3,259},{259,3},{4... | collective-permute-start | bytes 294920 | tf_op jit(solution)/shard_map/ppermute | solution.py:242
  13.0 2.9 %collective-permute-done = bf16[2,3,64,128]{3,2,1,0:T(8,128)(2,1)S(1)} collective-permute-done((bf16[2,3,64,128]{3,2,1,0:T(8,128)(2,1)S(1)}, bf16[2,3,64,128]{3,2,1,0:T(8,128)(2,1)S(1)}, u32[]{:S(2)}, u32[]{:S(2)}) %collective-permute-start) | collective-permute-done | bytes 98336 | tf_op jit(solution)/shard_map/ppermute | solution.py:242
  17.0 7.1 %all-to-all-start = ((bf16[8,3,2,64,128]{4,3,2,1,0:T(8,128)(2,1)}), bf16[8,3,2,64,128]{4,3,2,1,0:T(8,128)(2,1)S(1)}, u32[]{:S(2)}, u32[]{:S(2)}) async-start(bf16[8,3,2,64,128]{4,3,2,1,0:T(8,128)(2,1)} %bitcast.7), calls=%async_computation | async-start | bytes 1572864 | tf_op jit(solution)/shard_map/all_to_all | solution.py:25
  24.2 3.9 %collective-permute-start.1 = (bf16[8,512]{1,0:T(8,128)(2,1)S(1)}, bf16[8,512]{1,0:T(8,128)(2,1)S(1)}, u32[]{:S(2)}, u32[]{:S(2)}) collective-permute-start(bf16[8,512]{1,0:T(8,128)(2,1)S(1)} %slice.10), channel_id=1, source_target_pairs={{0,8},{8,16},{16,24},{24,32},{32,40},{40,48},{48,56},{56,64},{64,7... | collective-permute-start | bytes 24584 | tf_op jit(solution)/shard_map/ppermute | solution.py:237
  28.1 12.5 %collective-permute-done.1 = bf16[8,512]{1,0:T(8,128)(2,1)S(1)} collective-permute-done((bf16[8,512]{1,0:T(8,128)(2,1)S(1)}, bf16[8,512]{1,0:T(8,128)(2,1)S(1)}, u32[]{:S(2)}, u32[]{:S(2)}) %collective-permute-start.1) | collective-permute-done | bytes 8224 | tf_op jit(solution)/shard_map/ppermute | solution.py:237
  40.5 8.2 %collective-permute-start.2 = (bf16[1,136,512]{2,1,0:T(8,128)(2,1)S(1)}, bf16[1,136,512]{2,1,0:T(8,128)(2,1)}, u32[]{:S(2)}, u32[]{:S(2)}) collective-permute-start(bf16[1,136,512]{2,1,0:T(8,128)(2,1)S(1)} %maximum_bitcast_fusion), channel_id=1, source_target_pairs={{0,256},{2,258},{4,260},{6,262},{256,0},{258,2},{260,4},{262,6},{1... | collective-permute-start | bytes 417800 | tf_op jit(solution)/shard_map/ppermute | solution.py:242
  51.5 5.1 %all-to-all-start.1 = ((bf16[4,8,2,2,64,128]{5,4,3,2,1,0:T(8,128)(2,1)}), bf16[4,8,2,2,64,128]{5,4,3,2,1,0:T(8,128)(2,1)S(1)}, u32[]{:S(2)}, u32[]{:S(2)}) async-start(bf16[4,8,2,2,64,128]{5,4,3,2,1,0:T(8,128)(2,1)} %broadcast_in_dim.11), calls=%async_computation.1 | async-start | bytes 4194304 | tf_op jit(solution)/shard_map/all_to_all | solution.py:25
  57.5 7.1 %collective-permute-start.3 = (bf16[2,136,512]{2,1,0:T(8,128)(2,1)S(1)}, bf16[2,136,512]{2,1,0:T(8,128)(2,1)S(1)}, u32[]{:S(2)}, u32[]{:S(2)}) collective-permute-start(bf16[2,136,512]{2,1,0:T(8,128)(2,1)S(1)} %pad_maximum_fusion.refs_1_.refs_4_), channel_id=1, source_target_pairs={{0,4},{2,6},{4,0},{6,2},{256,260},{258,262},{260,256},{262,258},{1... | collective-permute-start | bytes 835592 | tf_op jit(solution)/shard_map/ppermute | solution.py:242
  64.7 8.6 %collective-permute-done.3.refs_2_.refs_5_ = bf16[2,136,512]{2,1,0:T(8,128)(2,1)S(1)} collective-permute-done((bf16[2,136,512]{2,1,0:T(8,128)(2,1)S(1)}, bf16[2,136,512]{2,1,0:T(8,128)(2,1)S(1)}, u32[]{:S(2)}, u32[]{:S(2)}) %collective-permute-start.3) | collective-permute-done | bytes 278560 | tf_op jit(solution)/shard_map/ppermute | solution.py:242
  75.2 3.9 %collective-permute-start.10 = (bf16[2,136,512]{2,1,0:T(8,128)(2,1)S(1)}, bf16[2,136,512]{2,1,0:T(8,128)(2,1)S(1)}, u32[]{:S(2)}, u32[]{:S(2)}) collective-permute-start(bf16[2,136,512]{2,1,0:T(8,128)(2,1)S(1)} %pad_maximum_fusion.refs_1_.refs_4_), channel_id=1, source_target_pairs={{0,2},{2,0},{4,6},{6,4},{256,258},{258,256},{260,262},{262,260},{1... | collective-permute-start | bytes 835592 | tf_op jit(solution)/shard_map/ppermute | solution.py:242
  81.0 3.6 %collective-permute-done.4.refs_4_.refs_7_ = bf16[2,136,512]{2,1,0:T(8,128)(2,1)S(1)} collective-permute-done((bf16[2,136,512]{2,1,0:T(8,128)(2,1)S(1)}, bf16[2,136,512]{2,1,0:T(8,128)(2,1)S(1)}, u32[]{:S(2)}, u32[]{:S(2)}) %collective-permute-start.4) | collective-permute-done | bytes 278560 | tf_op jit(solution)/shard_map/ppermute | solution.py:242
  88.5 3.9 %collective-permute-start.12 = (bf16[2,136,512]{2,1,0:T(8,128)(2,1)S(1)}, bf16[2,136,512]{2,1,0:T(8,128)(2,1)S(1)}, u32[]{:S(2)}, u32[]{:S(2)}) collective-permute-start(bf16[2,136,512]{2,1,0:T(8,128)(2,1)S(1)} %collective-permute-done.3.refs_2_.refs_5_), channel_id=1, source_target_pairs={{0,8},{8,0},{1,9},{9,1},{2,10},{10,2},{3,11},{11,3},{4,12},{12,4},... | collective-permute-start | bytes 835592 | tf_op jit(solution)/shard_map/ppermute | solution.py:242
  96.5 2.2 %collective-permute-start.6 = (bf16[2,136,512]{2,1,0:T(8,128)(2,1)S(1)}, bf16[2,136,512]{2,1,0:T(8,128)(2,1)S(1)}, u32[]{:S(2)}, u32[]{:S(2)}) collective-permute-start(bf16[2,136,512]{2,1,0:T(8,128)(2,1)S(1)} %collective-permute-done.5.refs_8_.refs_11_), channel_id=1, source_target_pairs={{0,1},{1,0},{2,3},{3,2},{4,5},{5,4},{6,7},{7,6},{8,9},{9,8},{10,11... | collective-permute-start | bytes 835592 | tf_op jit(solution)/shard_map/ppermute | solution.py:242
  103.1 2.6 %collective-permute-done.13.refs_7_.refs_10_ = bf16[2,136,512]{2,1,0:T(8,128)(2,1)S(1)} collective-permute-done((bf16[2,136,512]{2,1,0:T(8,128)(2,1)S(1)}, bf16[2,136,512]{2,1,0:T(8,128)(2,1)S(1)}, u32[]{:S(2)}, u32[]{:S(2)}) %collective-permute-start.13) | collective-permute-done | bytes 278560 | tf_op jit(solution)/shard_map/ppermute | solution.py:242
  107.6 2.4 %collective-permute-start.19 = (bf16[2,136,512]{2,1,0:T(8,128)(2,1)S(1)}, bf16[2,136,512]{2,1,0:T(8,128)(2,1)S(1)}, u32[]{:S(2)}, u32[]{:S(2)}) collective-permute-start(bf16[2,136,512]{2,1,0:T(8,128)(2,1)S(1)} %collective-permute-done.12.refs_6_.refs_9_), channel_id=1, source_target_pairs={{0,1},{1,0},{2,3},{3,2},{4,5},{5,4},{6,7},{7,6},{8,9},{9,8},{10,11... | collective-permute-start | bytes 835592 | tf_op jit(solution)/shard_map/ppermute | solution.py:242
  114.5 5.4 %shard_map.92 = bf16[16,4,8,128]{3,2,1,0:T(8,128)(2,1)} custom-call(s32[5]{0:T(128)S(1)} %stack.32.where, bf16[4,8,2,2,64,128]{5,4,3,2,1,0:T(8,128)(2,1)S(1)} %all-to-all-done.1.refs_0_, bf16[2,136,512]{2,1,0:T(8,128)(2,1)} %copy-done.4, bf16[2,136,512]{2,1,0:T(8,128)(2,1)} %copy-done.5, bf16[2,136,512]{2,1,0:T(8,128)(2,1)} %copy-done.7, ...), custom_call_target="tpu_custom_call" | custom-call | flops 1140850688 | bytes 6558228 | tf_op jit(solution)/shard_map/pallas_call | solution.py:224
  119.9 11.3 %all-to-all-start.2 = ((bf16[16,4,8,128]{3,2,1,0:T(8,128)(2,1)}), bf16[16,4,8,128]{3,2,1,0:T(8,128)(2,1)S(1)}, u32[]{:S(2)}, u32[]{:S(2)}) async-start(bf16[16,4,8,128]{3,2,1,0:T(8,128)(2,1)} %shard_map.92), calls=%async_computation.2 | async-start | bytes 262144 | tf_op jit(solution)/shard_map/all_to_all | solution.py:25
  131.3 2.8 %collective-permute-start.7 = (bf16[8,2,64,128]{3,2,1,0:T(8,128)(2,1)S(1)}, bf16[8,2,64,128]{3,2,1,0:T(8,128)(2,1)S(1)}, u32[]{:S(2)}, u32[]{:S(2)}) collective-permute-start(bf16[8,2,64,128]{3,2,1,0:T(8,128)(2,1)S(1)} %slice_bitcast_fusion.refs_0_), channel_id=1, source_target_pairs={{0,64},{64,0},{128,192},{192,128},{1,65},{65,1},{129,193},{193,129... | collective-permute-start | bytes 786440 | tf_op jit(solution)/shard_map/ppermute | solution.py:242
  134.0 2.6 %collective-permute-start.8 = (bf16[8,2,64,128]{3,2,1,0:T(8,128)(2,1)S(1)}, bf16[8,2,64,128]{3,2,1,0:T(8,128)(2,1)S(1)}, u32[]{:S(2)}, u32[]{:S(2)}) collective-permute-start(bf16[8,2,64,128]{3,2,1,0:T(8,128)(2,1)S(1)} %slice_bitcast_fusion.refs_0_), channel_id=1, source_target_pairs={{0,128},{64,192},{128,0},{192,64},{1,129},{65,193},{129,1},{193,65... | collective-permute-start | bytes 786440 | tf_op jit(solution)/shard_map/ppermute | solution.py:242
  136.7 5.0 %collective-permute-start.9 = (bf16[8,2,64,128]{3,2,1,0:T(8,128)(2,1)S(1)}, bf16[8,2,64,128]{3,2,1,0:T(8,128)(2,1)}, u32[]{:S(2)}, u32[]{:S(2)}) collective-permute-start(bf16[8,2,64,128]{3,2,1,0:T(8,128)(2,1)S(1)} %slice_bitcast_fusion.refs_0_), channel_id=1, source_target_pairs={{0,192},{64,128},{128,64},{192,0},{1,193},{65,129},{129,65},{193,1... | collective-permute-start | bytes 786440 | tf_op jit(solution)/shard_map/ppermute | solution.py:242
  144.6 9.3 %all-to-all-start.3 = ((bf16[16,4,8,128]{3,2,1,0:T(8,128)(2,1)}), bf16[16,4,8,128]{3,2,1,0:T(8,128)(2,1)S(1)}, u32[]{:S(2)}, u32[]{:S(2)}) async-start(bf16[16,4,8,128]{3,2,1,0:T(8,128)(2,1)} %bitcast.11), calls=%async_computation.3 | async-start | bytes 262144 | tf_op jit(solution)/shard_map/all_to_all | solution.py:25
  154.0 4.5 %shard_map.95.query = bf16[4,128,128]{2,1,0:T(8,128)(2,1)S(1)} custom-call(s32[5]{0:T(128)S(1)} %stack.32.where, bf16[8,2,64,128]{3,2,1,0:T(8,128)(2,1)S(1)} %slice_bitcast_fusion.refs_0_, bf16[8,2,64,128]{3,2,1,0:T(8,128)(2,1)S(1)} %collective-permute-done.7.refs_1_, bf16[8,2,64,128]{3,2,1,0:T(8,128)(2,1)S(1)} %collective-permute-done.8.refs_2_, ...), custom_call_target="tpu_custom_call" | custom-call | flops 570425344 | bytes 5509652 | tf_op jit(solution)/shard_map/pallas_call | solution.py:224
  158.4 4.1 %all-to-all-done.3.returned = bf16[16,4,8,128]{3,2,1,0:T(8,128)(2,1)S(1)} async-done(((bf16[16,4,8,128]{3,2,1,0:T(8,128)(2,1)}), bf16[16,4,8,128]{3,2,1,0:T(8,128)(2,1)S(1)}, u32[]{:S(2)}, u32[]{:S(2)}) %all-to-all-start.3) | async-done | bytes 131104 | tf_op jit(solution)/shard_map/all_to_all | solution.py:25
  162.6 13.3 %all_to_all.25.gated = bf16[4,128,128]{2,1,0:T(8,128)(2,1)S(1)} all-to-all(bf16[4,128,128]{2,1,0:T(8,128)(2,1)S(1)} %shard_map.96), channel_id=1, replica_groups=mesh['z_hi'=2,'x'=4,'yh'=4,'yl'=2,'z_lo'=4,'core'=2] {'z_hi','yl'}, dimensions={0} | all-to-all | bytes 262144 | tf_op jit(solution)/shard_map/all_to_all | solution.py:25
  (89 shorter events, 33.0 us)
Async XLA Ops:
  2.1 13.8 %collective-permute-start = (bf16[2,3,64,128]{3,2,1,0:T(8,128)(2,1)S(1)}, bf16[2,3,64,128]{3,2,1,0:T(8,128)(2,1)S(1)}, u32[]{:S(2)}, u32[]{:S(2)}) collective-permute-start(bf16[2,3,64,128]{3,2,1,0:T(8,128)(2,1)S(1)} %get-tuple-element.20), channel_id=1, source_target_pairs={{0,256},{256,0},{1,257},{257,1},{2,258},{258,2},{3,259},{259,3},{4... | collective-permute-start | bytes 294920 | tf_op jit(solution)/shard_map/ppermute | solution.py:242
  17.0 32.5 %all-to-all-start = ((bf16[8,3,2,64,128]{4,3,2,1,0:T(8,128)(2,1)}), bf16[8,3,2,64,128]{4,3,2,1,0:T(8,128)(2,1)S(1)}, u32[]{:S(2)}, u32[]{:S(2)}) async-start(bf16[8,3,2,64,128]{4,3,2,1,0:T(8,128)(2,1)} %bitcast.7), calls=%async_computation | async-start | bytes 1572864 | tf_op jit(solution)/shard_map/all_to_all | solution.py:25
  24.2 16.4 %collective-permute-start.1 = (bf16[8,512]{1,0:T(8,128)(2,1)S(1)}, bf16[8,512]{1,0:T(8,128)(2,1)S(1)}, u32[]{:S(2)}, u32[]{:S(2)}) collective-permute-start(bf16[8,512]{1,0:T(8,128)(2,1)S(1)} %slice.10), channel_id=1, source_target_pairs={{0,8},{8,16},{16,24},{24,32},{32,40},{40,48},{48,56},{56,64},{64,7... | collective-permute-start | bytes 24584 | tf_op jit(solution)/shard_map/ppermute | solution.py:237
  40.5 16.0 %collective-permute-start.2 = (bf16[1,136,512]{2,1,0:T(8,128)(2,1)S(1)}, bf16[1,136,512]{2,1,0:T(8,128)(2,1)}, u32[]{:S(2)}, u32[]{:S(2)}) collective-permute-start(bf16[1,136,512]{2,1,0:T(8,128)(2,1)S(1)} %maximum_bitcast_fusion), channel_id=1, source_target_pairs={{0,256},{2,258},{4,260},{6,262},{256,0},{258,2},{260,4},{262,6},{1... | collective-permute-start | bytes 417800 | tf_op jit(solution)/shard_map/ppermute | solution.py:242
  51.5 63.0 %all-to-all-start.1 = ((bf16[4,8,2,2,64,128]{5,4,3,2,1,0:T(8,128)(2,1)}), bf16[4,8,2,2,64,128]{5,4,3,2,1,0:T(8,128)(2,1)S(1)}, u32[]{:S(2)}, u32[]{:S(2)}) async-start(bf16[4,8,2,2,64,128]{5,4,3,2,1,0:T(8,128)(2,1)} %broadcast_in_dim.11), calls=%async_computation.1 | async-start | bytes 4194304 | tf_op jit(solution)/shard_map/all_to_all | solution.py:25
  57.5 15.7 %collective-permute-start.3 = (bf16[2,136,512]{2,1,0:T(8,128)(2,1)S(1)}, bf16[2,136,512]{2,1,0:T(8,128)(2,1)S(1)}, u32[]{:S(2)}, u32[]{:S(2)}) collective-permute-start(bf16[2,136,512]{2,1,0:T(8,128)(2,1)S(1)} %pad_maximum_fusion.refs_1_.refs_4_), channel_id=1, source_target_pairs={{0,4},{2,6},{4,0},{6,2},{256,260},{258,262},{260,256},{262,258},{1... | collective-permute-start | bytes 835592 | tf_op jit(solution)/shard_map/ppermute | solution.py:242
  73.2 11.4 %collective-permute-start.4 = (bf16[2,136,512]{2,1,0:T(8,128)(2,1)S(1)}, bf16[2,136,512]{2,1,0:T(8,128)(2,1)S(1)}, u32[]{:S(2)}, u32[]{:S(2)}) collective-permute-start(bf16[2,136,512]{2,1,0:T(8,128)(2,1)S(1)} %collective-permute-done.3.refs_2_.refs_5_), channel_id=1, source_target_pairs={{0,2},{2,0},{4,6},{6,4},{256,258},{258,256},{260,262},{262,260},{1... | collective-permute-start | bytes 835592 | tf_op jit(solution)/shard_map/ppermute | solution.py:242
  75.2 17.3 %collective-permute-start.10 = (bf16[2,136,512]{2,1,0:T(8,128)(2,1)S(1)}, bf16[2,136,512]{2,1,0:T(8,128)(2,1)S(1)}, u32[]{:S(2)}, u32[]{:S(2)}) collective-permute-start(bf16[2,136,512]{2,1,0:T(8,128)(2,1)S(1)} %pad_maximum_fusion.refs_1_.refs_4_), channel_id=1, source_target_pairs={{0,2},{2,0},{4,6},{6,4},{256,258},{258,256},{260,262},{262,260},{1... | collective-permute-start | bytes 835592 | tf_op jit(solution)/shard_map/ppermute | solution.py:242
  79.1 15.3 %collective-permute-start.11 = (bf16[2,136,512]{2,1,0:T(8,128)(2,1)S(1)}, bf16[2,136,512]{2,1,0:T(8,128)(2,1)S(1)}, u32[]{:S(2)}, u32[]{:S(2)}) collective-permute-start(bf16[2,136,512]{2,1,0:T(8,128)(2,1)S(1)} %pad_maximum_fusion.refs_1_.refs_4_), channel_id=1, source_target_pairs={{0,8},{8,0},{1,9},{9,1},{2,10},{10,2},{3,11},{11,3},{4,12},{12,4},... | collective-permute-start | bytes 835592 | tf_op jit(solution)/shard_map/ppermute | solution.py:242
  84.6 11.9 %collective-permute-start.5 = (bf16[2,136,512]{2,1,0:T(8,128)(2,1)S(1)}, bf16[2,136,512]{2,1,0:T(8,128)(2,1)S(1)}, u32[]{:S(2)}, u32[]{:S(2)}) collective-permute-start(bf16[2,136,512]{2,1,0:T(8,128)(2,1)S(1)} %collective-permute-done.4.refs_4_.refs_7_), channel_id=1, source_target_pairs={{0,8},{8,0},{1,9},{9,1},{2,10},{10,2},{3,11},{11,3},{4,12},{12,4},... | collective-permute-start | bytes 835592 | tf_op jit(solution)/shard_map/ppermute | solution.py:242
  86.6 12.2 %collective-permute-start.14 = (bf16[2,136,512]{2,1,0:T(8,128)(2,1)S(1)}, bf16[2,136,512]{2,1,0:T(8,128)(2,1)S(1)}, u32[]{:S(2)}, u32[]{:S(2)}) collective-permute-start(bf16[2,136,512]{2,1,0:T(8,128)(2,1)S(1)} %pad_maximum_fusion.refs_1_.refs_4_), channel_id=1, source_target_pairs={{0,1},{1,0},{2,3},{3,2},{4,5},{5,4},{6,7},{7,6},{8,9},{9,8},{10,11... | collective-permute-start | bytes 835592 | tf_op jit(solution)/shard_map/ppermute | solution.py:242
  88.5 12.4 %collective-permute-start.12 = (bf16[2,136,512]{2,1,0:T(8,128)(2,1)S(1)}, bf16[2,136,512]{2,1,0:T(8,128)(2,1)S(1)}, u32[]{:S(2)}, u32[]{:S(2)}) collective-permute-start(bf16[2,136,512]{2,1,0:T(8,128)(2,1)S(1)} %collective-permute-done.3.refs_2_.refs_5_), channel_id=1, source_target_pairs={{0,8},{8,0},{1,9},{9,1},{2,10},{10,2},{3,11},{11,3},{4,12},{12,4},... | collective-permute-start | bytes 835592 | tf_op jit(solution)/shard_map/ppermute | solution.py:242
  92.4 13.3 %collective-permute-start.13 = (bf16[2,136,512]{2,1,0:T(8,128)(2,1)S(1)}, bf16[2,136,512]{2,1,0:T(8,128)(2,1)S(1)}, u32[]{:S(2)}, u32[]{:S(2)}) collective-permute-start(bf16[2,136,512]{2,1,0:T(8,128)(2,1)S(1)} %collective-permute-done.10.refs_3_.refs_6_), channel_id=1, source_target_pairs={{0,8},{8,0},{1,9},{9,1},{2,10},{10,2},{3,11},{11,3},{4,12},{12,4},... | collective-permute-start | bytes 835592 | tf_op jit(solution)/shard_map/ppermute | solution.py:242
  94.4 13.2 %collective-permute-start.15 = (bf16[2,136,512]{2,1,0:T(8,128)(2,1)S(1)}, bf16[2,136,512]{2,1,0:T(8,128)(2,1)S(1)}, u32[]{:S(2)}, u32[]{:S(2)}) collective-permute-start(bf16[2,136,512]{2,1,0:T(8,128)(2,1)S(1)} %collective-permute-done.3.refs_2_.refs_5_), channel_id=1, source_target_pairs={{0,1},{1,0},{2,3},{3,2},{4,5},{5,4},{6,7},{7,6},{8,9},{9,8},{10,11... | collective-permute-start | bytes 835592 | tf_op jit(solution)/shard_map/ppermute | solution.py:242
  96.5 13.5 %collective-permute-start.6 = (bf16[2,136,512]{2,1,0:T(8,128)(2,1)S(1)}, bf16[2,136,512]{2,1,0:T(8,128)(2,1)S(1)}, u32[]{:S(2)}, u32[]{:S(2)}) collective-permute-start(bf16[2,136,512]{2,1,0:T(8,128)(2,1)S(1)} %collective-permute-done.5.refs_8_.refs_11_), channel_id=1, source_target_pairs={{0,1},{1,0},{2,3},{3,2},{4,5},{5,4},{6,7},{7,6},{8,9},{9,8},{10,11... | collective-permute-start | bytes 835592 | tf_op jit(solution)/shard_map/ppermute | solution.py:242
  98.8 14.1 %collective-permute-start.16 = (bf16[2,136,512]{2,1,0:T(8,128)(2,1)S(1)}, bf16[2,136,512]{2,1,0:T(8,128)(2,1)S(1)}, u32[]{:S(2)}, u32[]{:S(2)}) collective-permute-start(bf16[2,136,512]{2,1,0:T(8,128)(2,1)S(1)} %collective-permute-done.10.refs_3_.refs_6_), channel_id=1, source_target_pairs={{0,1},{1,0},{2,3},{3,2},{4,5},{5,4},{6,7},{7,6},{8,9},{9,8},{10,11... | collective-permute-start | bytes 835592 | tf_op jit(solution)/shard_map/ppermute | solution.py:242
  100.9 11.9 %collective-permute-start.18 = (bf16[2,136,512]{2,1,0:T(8,128)(2,1)S(1)}, bf16[2,136,512]{2,1,0:T(8,128)(2,1)S(1)}, u32[]{:S(2)}, u32[]{:S(2)}) collective-permute-start(bf16[2,136,512]{2,1,0:T(8,128)(2,1)S(1)} %collective-permute-done.11.refs_5_.refs_8_), channel_id=1, source_target_pairs={{0,1},{1,0},{2,3},{3,2},{4,5},{5,4},{6,7},{7,6},{8,9},{9,8},{10,11... | collective-permute-start | bytes 835592 | tf_op jit(solution)/shard_map/ppermute | solution.py:242
  105.7 7.2 %collective-permute-start.17 = (bf16[2,136,512]{2,1,0:T(8,128)(2,1)S(1)}, bf16[2,136,512]{2,1,0:T(8,128)(2,1)S(1)}, u32[]{:S(2)}, u32[]{:S(2)}) collective-permute-start(bf16[2,136,512]{2,1,0:T(8,128)(2,1)S(1)} %collective-permute-done.4.refs_4_.refs_7_), channel_id=1, source_target_pairs={{0,1},{1,0},{2,3},{3,2},{4,5},{5,4},{6,7},{7,6},{8,9},{9,8},{10,11... | collective-permute-start | bytes 835592 | tf_op jit(solution)/shard_map/ppermute | solution.py:242
  107.6 5.3 %collective-permute-start.19 = (bf16[2,136,512]{2,1,0:T(8,128)(2,1)S(1)}, bf16[2,136,512]{2,1,0:T(8,128)(2,1)S(1)}, u32[]{:S(2)}, u32[]{:S(2)}) collective-permute-start(bf16[2,136,512]{2,1,0:T(8,128)(2,1)S(1)} %collective-permute-done.12.refs_6_.refs_9_), channel_id=1, source_target_pairs={{0,1},{1,0},{2,3},{3,2},{4,5},{5,4},{6,7},{7,6},{8,9},{9,8},{10,11... | collective-permute-start | bytes 835592 | tf_op jit(solution)/shard_map/ppermute | solution.py:242
  119.9 22.6 %all-to-all-start.2 = ((bf16[16,4,8,128]{3,2,1,0:T(8,128)(2,1)}), bf16[16,4,8,128]{3,2,1,0:T(8,128)(2,1)S(1)}, u32[]{:S(2)}, u32[]{:S(2)}) async-start(bf16[16,4,8,128]{3,2,1,0:T(8,128)(2,1)} %shard_map.92), calls=%async_computation.2 | async-start | bytes 262144 | tf_op jit(solution)/shard_map/all_to_all | solution.py:25
  131.3 22.7 %collective-permute-start.7 = (bf16[8,2,64,128]{3,2,1,0:T(8,128)(2,1)S(1)}, bf16[8,2,64,128]{3,2,1,0:T(8,128)(2,1)S(1)}, u32[]{:S(2)}, u32[]{:S(2)}) collective-permute-start(bf16[8,2,64,128]{3,2,1,0:T(8,128)(2,1)S(1)} %slice_bitcast_fusion.refs_0_), channel_id=1, source_target_pairs={{0,64},{64,0},{128,192},{192,128},{1,65},{65,1},{129,193},{193,129... | collective-permute-start | bytes 786440 | tf_op jit(solution)/shard_map/ppermute | solution.py:242
  134.0 19.9 %collective-permute-start.8 = (bf16[8,2,64,128]{3,2,1,0:T(8,128)(2,1)S(1)}, bf16[8,2,64,128]{3,2,1,0:T(8,128)(2,1)S(1)}, u32[]{:S(2)}, u32[]{:S(2)}) collective-permute-start(bf16[8,2,64,128]{3,2,1,0:T(8,128)(2,1)S(1)} %slice_bitcast_fusion.refs_0_), channel_id=1, source_target_pairs={{0,128},{64,192},{128,0},{192,64},{1,129},{65,193},{129,1},{193,65... | collective-permute-start | bytes 786440 | tf_op jit(solution)/shard_map/ppermute | solution.py:242
  136.7 17.3 %collective-permute-start.9 = (bf16[8,2,64,128]{3,2,1,0:T(8,128)(2,1)S(1)}, bf16[8,2,64,128]{3,2,1,0:T(8,128)(2,1)}, u32[]{:S(2)}, u32[]{:S(2)}) collective-permute-start(bf16[8,2,64,128]{3,2,1,0:T(8,128)(2,1)S(1)} %slice_bitcast_fusion.refs_0_), channel_id=1, source_target_pairs={{0,192},{64,128},{128,64},{192,0},{1,193},{65,129},{129,65},{193,1... | collective-permute-start | bytes 786440 | tf_op jit(solution)/shard_map/ppermute | solution.py:242
  144.6 17.9 %all-to-all-start.3 = ((bf16[16,4,8,128]{3,2,1,0:T(8,128)(2,1)}), bf16[16,4,8,128]{3,2,1,0:T(8,128)(2,1)S(1)}, u32[]{:S(2)}, u32[]{:S(2)}) async-start(bf16[16,4,8,128]{3,2,1,0:T(8,128)(2,1)} %bitcast.11), calls=%async_computation.3 | async-start | bytes 262144 | tf_op jit(solution)/shard_map/all_to_all | solution.py:25
  (22 other events, 402.8 us)

commit v2 on v0

--- a/solution.py
+++ b/solution.py
@@ -257,6 +257,7 @@
         (pltpu.VMEM((3, 64, 512), BF16), pltpu.SemaphoreType.DMA((3,))),
         in_specs=[smem] + [anywhere] * 3,
     )
+    others, halo = lax.optimization_barrier((others, halo))
     got = swapped(others, ("z_hi",), 1)
     first = from_everyone(jnp.stack([own, got], axis=2), ("yh",), ("yl",))
 
@@ -275,12 +276,9 @@
     even_y = swapped(even, ("yl",), 1)
     odd_y = swapped(odd, ("yl",), 1)
     ours = (even, odd, even_y, odd_y)
-    features = list(ours)
-    for blocks in ours:
-        features.append(swapped(blocks, ("core",), 1))
-    slice_of_first, last = lax.optimization_barrier((first[:, 2], features[-1]))
-    features = (*features[:-1], last)
-    query_weights = [slice_of_first]
+    features = [swapped(v, ("core",), 1) for v in ours]
+    features = (*ours, *features)
+    query_weights = [first[:, 2]]
     query_weights += [swapped(query_weights[0], ("x",), d) for d in (1, 2, 3)]
 
     kept = [pltpu.with_memory_space_constraint(v, pltpu.HBM) for v in features]

time: 185 us -> 168 us (0.908)
  waiting for transfers between devices: 56.9 us -> 36.6 us
  blocking collectives: 14.7 us -> 18.3 us
    ppermute x1, waiting for transfers between devices: 12.4 us -> 1.96 us  [of_previous(): return lax.ppermute(value, axes, [(i, i + 1) for i in range(count - 1)])]
    ppermute x13, waiting for transfers between devices: 40.5 us -> 30.6 us  [swapped(): return lax.ppermute(value, axes, [(i, i ^ bits) for i in range(count)])]
    all_to_all x1, blocking collectives: 14.7 us -> 18.3 us  [exchanged(): return lax.all_to_all(value, axes, split_axis=0, concat_axis=0, tiled=True)]
    all_to_all x4, starting transfers between devices: 34.2 us -> 31.8 us  [exchanged(): return lax.all_to_all(value, axes, split_axis=0, concat_axis=0, tiled=True)]
  transfers between devices with their start and end apart: 18 -> 18, of which waited for: 9 -> 8; matrix products, arithmetic and copies ran while one was open for 2% -> 2% of each run, Pallas kernels for 4% -> 6%
where the time goes in v2:
time: 168 us; the launch traced here: 165 us
  starting transfers between devices  86.8 us (52%)
  waiting for transfers between devices  36.6 us (22%)
  blocking collectives  18.3 us (11%)
  Pallas kernels  15.7 us (9%)
  local copies, waits for them, and re-layouts  7.45 us (4%)
    ppermute x13, starting transfers between devices, swapped(): return lax.ppermute(value, axes, [(i, i ^ bits) for i in range(count)])  51.5 us
    all_to_all x4, starting transfers between devices, exchanged(): return lax.all_to_all(value, axes, split_axis=0, concat_axis=0, tiled=True)  31.8 us
    ppermute x13, waiting for transfers between devices, swapped(): return lax.ppermute(value, axes, [(i, i ^ bits) for i in range(count)])  30.6 us
    all_to_all x1, blocking collectives, exchanged(): return lax.all_to_all(value, axes, split_axis=0, concat_axis=0, tiled=True)  18.3 us
    pallas_call x7, Pallas kernels, call(): pl.pallas_call(kernel, out_shape=out_shape, in_specs=specs, out_specs=jax...  15.7 us
    all_to_all x4, waiting for transfers between devices, exchanged(): return lax.all_to_all(value, axes, split_axis=0, concat_axis=0, tiled=True)  4.04 us
    ppermute x1, starting transfers between devices, of_previous(): return lax.ppermute(value, axes, [(i, i + 1) for i in range(count - 1)])  3.47 us
  transfers between devices with their start and end apart: 18, of which 8 were waited for; matrix products, arithmetic and copies ran while one was open for 2% of the time, Pallas kernels for 6%

profile of v2, /device:TPU:6, one launch (start us, length us, event | category | flops | bytes accessed | tf_op | source)
XLA Modules:
  0.0 165.4 jit_solution(12106846482940596214)
XLA Ops:
  0.8 3.5 %collective-permute-start = (bf16[8,512]{1,0:T(8,128)(2,1)S(1)}, bf16[8,512]{1,0:T(8,128)(2,1)S(1)}, u32[]{:S(2)}, u32[]{:S(2)}) collective-permute-start(bf16[8,512]{1,0:T(8,128)(2,1)S(1)} %slice.9), channel_id=1, source_target_pairs={{0,8},{8,16},{16,24},{24,32},{32,40},{40,48},{48,56},{56,64},{64,7... | collective-permute-start | bytes 24584 | tf_op jit(solution)/shard_map/ppermute | solution.py:234
  8.4 10.9 %collective-permute-start.1 = (bf16[2,3,64,128]{3,2,1,0:T(8,128)(2,1)S(1)}, bf16[2,3,64,128]{3,2,1,0:T(8,128)(2,1)S(1)}, u32[]{:S(2)}, u32[]{:S(2)}) collective-permute-start(bf16[2,3,64,128]{3,2,1,0:T(8,128)(2,1)S(1)} %get-tuple-element.21), channel_id=1, source_target_pairs={{0,256},{256,0},{1,257},{257,1},{2,258},{258,2},{3,259},{259,3},{4... | collective-permute-start | bytes 294920 | tf_op jit(solution)/shard_map/ppermute | solution.py:239
  19.3 3.2 %collective-permute-done.1 = bf16[2,3,64,128]{3,2,1,0:T(8,128)(2,1)S(1)} collective-permute-done((bf16[2,3,64,128]{3,2,1,0:T(8,128)(2,1)S(1)}, bf16[2,3,64,128]{3,2,1,0:T(8,128)(2,1)S(1)}, u32[]{:S(2)}, u32[]{:S(2)}) %collective-permute-start.1) | collective-permute-done | bytes 98336 | tf_op jit(solution)/shard_map/ppermute | solution.py:239
  23.7 6.8 %all-to-all-start = ((bf16[8,3,2,64,128]{4,3,2,1,0:T(8,128)(2,1)}), bf16[8,3,2,64,128]{4,3,2,1,0:T(8,128)(2,1)S(1)}, u32[]{:S(2)}, u32[]{:S(2)}) async-start(bf16[8,3,2,64,128]{4,3,2,1,0:T(8,128)(2,1)} %bitcast.7), calls=%async_computation | async-start | bytes 1572864 | tf_op jit(solution)/shard_map/all_to_all | solution.py:25
  30.5 7.7 %collective-permute-start.2 = (bf16[1,136,512]{2,1,0:T(8,128)(2,1)S(1)}, bf16[1,136,512]{2,1,0:T(8,128)(2,1)S(1)}, u32[]{:S(2)}, u32[]{:S(2)}) collective-permute-start(bf16[1,136,512]{2,1,0:T(8,128)(2,1)S(1)} %maximum_bitcast_fusion), channel_id=1, source_target_pairs={{0,256},{2,258},{4,260},{6,262},{256,0},{258,2},{260,4},{262,6},{1... | collective-permute-start | bytes 417800 | tf_op jit(solution)/shard_map/ppermute | solution.py:239
  38.2 4.6 %collective-permute-done.2 = bf16[1,136,512]{2,1,0:T(8,128)(2,1)S(1)} collective-permute-done((bf16[1,136,512]{2,1,0:T(8,128)(2,1)S(1)}, bf16[1,136,512]{2,1,0:T(8,128)(2,1)S(1)}, u32[]{:S(2)}, u32[]{:S(2)}) %collective-permute-start.2) | collective-permute-done | bytes 139296 | tf_op jit(solution)/shard_map/ppermute | solution.py:239
  42.8 5.1 %collective-permute-start.3 = (bf16[2,136,512]{2,1,0:T(8,128)(2,1)S(1)}, bf16[2,136,512]{2,1,0:T(8,128)(2,1)S(1)}, u32[]{:S(2)}, u32[]{:S(2)}) collective-permute-start(bf16[2,136,512]{2,1,0:T(8,128)(2,1)S(1)} %pad_maximum_fusion.1), channel_id=1, source_target_pairs={{0,4},{2,6},{4,0},{6,2},{256,260},{258,262},{260,256},{262,258},{1... | collective-permute-start | bytes 835592 | tf_op jit(solution)/shard_map/ppermute | solution.py:239
  47.9 8.7 %collective-permute-done.3 = bf16[2,136,512]{2,1,0:T(8,128)(2,1)S(1)} collective-permute-done((bf16[2,136,512]{2,1,0:T(8,128)(2,1)S(1)}, bf16[2,136,512]{2,1,0:T(8,128)(2,1)S(1)}, u32[]{:S(2)}, u32[]{:S(2)}) %collective-permute-start.3) | collective-permute-done | bytes 278560 | tf_op jit(solution)/shard_map/ppermute | solution.py:239
  56.7 2.6 %collective-permute-start.7 = (bf16[4,136,512]{2,1,0:T(8,128)(2,1)S(1)}, bf16[4,136,512]{2,1,0:T(8,128)(2,1)}, u32[]{:S(2)}, u32[]{:S(2)}) collective-permute-start(bf16[4,136,512]{2,1,0:T(8,128)(2,1)S(1)} %pad_maximum_fusion.refs_1_.refs_4_), channel_id=1, source_target_pairs={{0,2},{2,0},{4,6},{6,4},{256,258},{258,256},{260,262},{262,260},{1... | collective-permute-start | bytes 1671176 | tf_op jit(solution)/shard_map/ppermute | solution.py:239
  62.1 6.1 %all-to-all-start.1 = ((bf16[4,8,2,2,64,128]{5,4,3,2,1,0:T(8,128)(2,1)}), bf16[4,8,2,2,64,128]{5,4,3,2,1,0:T(8,128)(2,1)S(1)}, u32[]{:S(2)}, u32[]{:S(2)}) async-start(bf16[4,8,2,2,64,128]{5,4,3,2,1,0:T(8,128)(2,1)} %broadcast_in_dim.11), calls=%async_computation.1 | async-start | bytes 4194304 | tf_op jit(solution)/shard_map/all_to_all | solution.py:25
  68.2 3.7 %collective-permute-start.8 = (bf16[4,136,512]{2,1,0:T(8,128)(2,1)S(1)}, bf16[4,136,512]{2,1,0:T(8,128)(2,1)S(1)}, u32[]{:S(2)}, u32[]{:S(2)}) collective-permute-start(bf16[4,136,512]{2,1,0:T(8,128)(2,1)S(1)} %pad_maximum_fusion.refs_1_.refs_4_), channel_id=1, source_target_pairs={{0,8},{8,0},{1,9},{9,1},{2,10},{10,2},{3,11},{11,3},{4,12},{12,4},... | collective-permute-start | bytes 1671176 | tf_op jit(solution)/shard_map/ppermute | solution.py:239
  71.9 3.0 %collective-permute-start.9 = (bf16[4,136,512]{2,1,0:T(8,128)(2,1)}, bf16[4,136,512]{2,1,0:T(8,128)(2,1)S(1)}, u32[]{:S(2)}, u32[]{:S(2)}) collective-permute-start(bf16[4,136,512]{2,1,0:T(8,128)(2,1)} %collective-permute-done.7.refs_2_.refs_5_), channel_id=1, source_target_pairs={{0,8},{8,0},{1,9},{9,1},{2,10},{10,2},{3,11},{11,3},{4,12},{12,4},... | collective-permute-start | bytes 1671176 | tf_op jit(solution)/shard_map/ppermute | solution.py:239
  76.8 2.4 %collective-permute-start.11 = (bf16[4,136,512]{2,1,0:T(8,128)(2,1)}, bf16[4,136,512]{2,1,0:T(8,128)(2,1)S(1)}, u32[]{:S(2)}, u32[]{:S(2)}) collective-permute-start(bf16[4,136,512]{2,1,0:T(8,128)(2,1)} %collective-permute-done.7.refs_2_.refs_5_), channel_id=1, source_target_pairs={{0,1},{1,0},{2,3},{3,2},{4,5},{5,4},{6,7},{7,6},{8,9},{9,8},{10,11... | collective-permute-start | bytes 1671176 | tf_op jit(solution)/shard_map/ppermute | solution.py:239
  79.2 6.5 %collective-permute-done.8.refs_3_.refs_6_ = bf16[4,136,512]{2,1,0:T(8,128)(2,1)S(1)} collective-permute-done((bf16[4,136,512]{2,1,0:T(8,128)(2,1)S(1)}, bf16[4,136,512]{2,1,0:T(8,128)(2,1)S(1)}, u32[]{:S(2)}, u32[]{:S(2)}) %collective-permute-start.8) | collective-permute-done | bytes 557088 | tf_op jit(solution)/shard_map/ppermute | solution.py:239
  87.7 7.3 %collective-permute-done.9.refs_4_.refs_7_ = bf16[4,136,512]{2,1,0:T(8,128)(2,1)S(1)} collective-permute-done((bf16[4,136,512]{2,1,0:T(8,128)(2,1)}, bf16[4,136,512]{2,1,0:T(8,128)(2,1)S(1)}, u32[]{:S(2)}, u32[]{:S(2)}) %collective-permute-start.9) | collective-permute-done | bytes 557088 | tf_op jit(solution)/shard_map/ppermute | solution.py:239
  98.9 5.4 %shard_map.92 = bf16[16,4,8,128]{3,2,1,0:T(8,128)(2,1)} custom-call(s32[5]{0:T(128)S(1)} %stack.32.where, bf16[4,8,2,2,64,128]{5,4,3,2,1,0:T(8,128)(2,1)S(1)} %all-to-all-done.1.refs_0_, bf16[4,136,512]{2,1,0:T(8,128)(2,1)} %copy-done.4, bf16[4,136,512]{2,1,0:T(8,128)(2,1)} %collective-permute-done.7.refs_2_.refs_5_, bf16[4,136,512]{2,1,0:T(8,128)(2,1)} %copy-done.6, ...), custom_call_target="tpu_custom_call" | custom-call | flops 1140850688 | bytes 6558228 | tf_op jit(solution)/shard_map/pallas_call | solution.py:221
  104.3 9.6 %all-to-all-start.2 = ((bf16[16,4,8,128]{3,2,1,0:T(8,128)(2,1)}), bf16[16,4,8,128]{3,2,1,0:T(8,128)(2,1)S(1)}, u32[]{:S(2)}, u32[]{:S(2)}) async-start(bf16[16,4,8,128]{3,2,1,0:T(8,128)(2,1)} %shard_map.92), calls=%async_computation.2 | async-start | bytes 262144 | tf_op jit(solution)/shard_map/all_to_all | solution.py:25
  114.9 2.8 %collective-permute-start.4 = (bf16[8,2,64,128]{3,2,1,0:T(8,128)(2,1)S(1)}, bf16[8,2,64,128]{3,2,1,0:T(8,128)(2,1)S(1)}, u32[]{:S(2)}, u32[]{:S(2)}) collective-permute-start(bf16[8,2,64,128]{3,2,1,0:T(8,128)(2,1)S(1)} %slice_bitcast_fusion.refs_0_), channel_id=1, source_target_pairs={{0,64},{64,0},{128,192},{192,128},{1,65},{65,1},{129,193},{193,129... | collective-permute-start | bytes 786440 | tf_op jit(solution)/shard_map/ppermute | solution.py:239
  117.7 2.6 %collective-permute-start.5 = (bf16[8,2,64,128]{3,2,1,0:T(8,128)(2,1)S(1)}, bf16[8,2,64,128]{3,2,1,0:T(8,128)(2,1)S(1)}, u32[]{:S(2)}, u32[]{:S(2)}) collective-permute-start(bf16[8,2,64,128]{3,2,1,0:T(8,128)(2,1)S(1)} %slice_bitcast_fusion.refs_0_), channel_id=1, source_target_pairs={{0,128},{64,192},{128,0},{192,64},{1,129},{65,193},{129,1},{193,65... | collective-permute-start | bytes 786440 | tf_op jit(solution)/shard_map/ppermute | solution.py:239
  120.3 5.0 %collective-permute-start.6 = (bf16[8,2,64,128]{3,2,1,0:T(8,128)(2,1)S(1)}, bf16[8,2,64,128]{3,2,1,0:T(8,128)(2,1)}, u32[]{:S(2)}, u32[]{:S(2)}) collective-permute-start(bf16[8,2,64,128]{3,2,1,0:T(8,128)(2,1)S(1)} %slice_bitcast_fusion.refs_0_), channel_id=1, source_target_pairs={{0,192},{64,128},{128,64},{192,0},{1,193},{65,129},{129,65},{193,1... | collective-permute-start | bytes 786440 | tf_op jit(solution)/shard_map/ppermute | solution.py:239
  128.2 9.3 %all-to-all-start.3 = ((bf16[16,4,8,128]{3,2,1,0:T(8,128)(2,1)}), bf16[16,4,8,128]{3,2,1,0:T(8,128)(2,1)S(1)}, u32[]{:S(2)}, u32[]{:S(2)}) async-start(bf16[16,4,8,128]{3,2,1,0:T(8,128)(2,1)} %bitcast.11), calls=%async_computation.3 | async-start | bytes 262144 | tf_op jit(solution)/shard_map/all_to_all | solution.py:25
  137.6 4.4 %shard_map.95.query = bf16[4,128,128]{2,1,0:T(8,128)(2,1)S(1)} custom-call(s32[5]{0:T(128)S(1)} %stack.32.where, bf16[8,2,64,128]{3,2,1,0:T(8,128)(2,1)S(1)} %slice_bitcast_fusion.refs_0_, bf16[8,2,64,128]{3,2,1,0:T(8,128)(2,1)S(1)} %collective-permute-done.4.refs_1_, bf16[8,2,64,128]{3,2,1,0:T(8,128)(2,1)S(1)} %collective-permute-done.5.refs_2_, ...), custom_call_target="tpu_custom_call" | custom-call | flops 570425344 | bytes 5509652 | tf_op jit(solution)/shard_map/pallas_call | solution.py:221
  142.0 4.0 %all-to-all-done.3.returned = bf16[16,4,8,128]{3,2,1,0:T(8,128)(2,1)S(1)} async-done(((bf16[16,4,8,128]{3,2,1,0:T(8,128)(2,1)}), bf16[16,4,8,128]{3,2,1,0:T(8,128)(2,1)S(1)}, u32[]{:S(2)}, u32[]{:S(2)}) %all-to-all-start.3) | async-done | bytes 131104 | tf_op jit(solution)/shard_map/all_to_all | solution.py:25
  146.1 18.3 %all_to_all.25.gated = bf16[4,128,128]{2,1,0:T(8,128)(2,1)S(1)} all-to-all(bf16[4,128,128]{2,1,0:T(8,128)(2,1)S(1)} %shard_map.96), channel_id=1, replica_groups=mesh['z_hi'=2,'x'=4,'yh'=4,'yl'=2,'z_lo'=4,'core'=2] {'z_hi','yl'}, dimensions={0} | all-to-all | bytes 262144 | tf_op jit(solution)/shard_map/all_to_all | solution.py:25
  (60 shorter events, 21.4 us)
Async XLA Ops:
  0.0 30.4 %copy-start.11 = (bf16[128,512]{1,0:T(8,128)(2,1)S(1)}, bf16[128,512]{1,0:T(8,128)(2,1)}, u32[]{:S(2)}) copy-start(bf16[128,512]{1,0:T(8,128)(2,1)} %param.9) | copy-start | bytes 393220
  0.8 7.6 %collective-permute-start = (bf16[8,512]{1,0:T(8,128)(2,1)S(1)}, bf16[8,512]{1,0:T(8,128)(2,1)S(1)}, u32[]{:S(2)}, u32[]{:S(2)}) collective-permute-start(bf16[8,512]{1,0:T(8,128)(2,1)S(1)} %slice.9), channel_id=1, source_target_pairs={{0,8},{8,16},{16,24},{24,32},{32,40},{40,48},{48,56},{56,64},{64,7... | collective-permute-start | bytes 24584 | tf_op jit(solution)/shard_map/ppermute | solution.py:234
  8.4 14.1 %collective-permute-start.1 = (bf16[2,3,64,128]{3,2,1,0:T(8,128)(2,1)S(1)}, bf16[2,3,64,128]{3,2,1,0:T(8,128)(2,1)S(1)}, u32[]{:S(2)}, u32[]{:S(2)}) collective-permute-start(bf16[2,3,64,128]{3,2,1,0:T(8,128)(2,1)S(1)} %get-tuple-element.21), channel_id=1, source_target_pairs={{0,256},{256,0},{1,257},{257,1},{2,258},{258,2},{3,259},{259,3},{4... | collective-permute-start | bytes 294920 | tf_op jit(solution)/shard_map/ppermute | solution.py:239
  22.6 36.8 %copy-start.12 = (f32[3,3,512]{2,1,0:T(4,128)S(1)}, f32[3,3,512]{2,1,0:T(4,128)}, u32[]{:S(2)}) copy-start(f32[3,3,512]{2,1,0:T(4,128)} %param.13) | copy-start | bytes 55300
  23.7 36.5 %all-to-all-start = ((bf16[8,3,2,64,128]{4,3,2,1,0:T(8,128)(2,1)}), bf16[8,3,2,64,128]{4,3,2,1,0:T(8,128)(2,1)S(1)}, u32[]{:S(2)}, u32[]{:S(2)}) async-start(bf16[8,3,2,64,128]{4,3,2,1,0:T(8,128)(2,1)} %bitcast.7), calls=%async_computation | async-start | bytes 1572864 | tf_op jit(solution)/shard_map/all_to_all | solution.py:25
  30.5 12.3 %collective-permute-start.2 = (bf16[1,136,512]{2,1,0:T(8,128)(2,1)S(1)}, bf16[1,136,512]{2,1,0:T(8,128)(2,1)S(1)}, u32[]{:S(2)}, u32[]{:S(2)}) collective-permute-start(bf16[1,136,512]{2,1,0:T(8,128)(2,1)S(1)} %maximum_bitcast_fusion), channel_id=1, source_target_pairs={{0,256},{2,258},{4,260},{6,262},{256,0},{258,2},{260,4},{262,6},{1... | collective-permute-start | bytes 417800 | tf_op jit(solution)/shard_map/ppermute | solution.py:239
  42.8 13.9 %collective-permute-start.3 = (bf16[2,136,512]{2,1,0:T(8,128)(2,1)S(1)}, bf16[2,136,512]{2,1,0:T(8,128)(2,1)S(1)}, u32[]{:S(2)}, u32[]{:S(2)}) collective-permute-start(bf16[2,136,512]{2,1,0:T(8,128)(2,1)S(1)} %pad_maximum_fusion.1), channel_id=1, source_target_pairs={{0,4},{2,6},{4,0},{6,2},{256,260},{258,262},{260,256},{262,258},{1... | collective-permute-start | bytes 835592 | tf_op jit(solution)/shard_map/ppermute | solution.py:239
  56.7 15.2 %collective-permute-start.7 = (bf16[4,136,512]{2,1,0:T(8,128)(2,1)S(1)}, bf16[4,136,512]{2,1,0:T(8,128)(2,1)}, u32[]{:S(2)}, u32[]{:S(2)}) collective-permute-start(bf16[4,136,512]{2,1,0:T(8,128)(2,1)S(1)} %pad_maximum_fusion.refs_1_.refs_4_), channel_id=1, source_target_pairs={{0,2},{2,0},{4,6},{6,4},{256,258},{258,256},{260,262},{262,260},{1... | collective-permute-start | bytes 1671176 | tf_op jit(solution)/shard_map/ppermute | solution.py:239
  62.1 36.8 %all-to-all-start.1 = ((bf16[4,8,2,2,64,128]{5,4,3,2,1,0:T(8,128)(2,1)}), bf16[4,8,2,2,64,128]{5,4,3,2,1,0:T(8,128)(2,1)S(1)}, u32[]{:S(2)}, u32[]{:S(2)}) async-start(bf16[4,8,2,2,64,128]{5,4,3,2,1,0:T(8,128)(2,1)} %broadcast_in_dim.11), calls=%async_computation.1 | async-start | bytes 4194304 | tf_op jit(solution)/shard_map/all_to_all | solution.py:25
  68.2 57.1 %copy-start = (bf16[832,256]{1,0:T(8,128)(2,1)S(1)}, bf16[832,256]{1,0:T(8,128)(2,1)}, u32[]{:S(2)}) copy-start(bf16[832,256]{1,0:T(8,128)(2,1)} %constant.145.tables) | copy-start | bytes 1277956
  68.2 57.1 %copy-start.1 = (f32[8,8192]{1,0:T(8,128)S(1)}, f32[8,8192]{1,0:T(8,128)}, u32[]{:S(2)}) copy-start(f32[8,8192]{1,0:T(8,128)} %filters) | copy-start | bytes 786436
  68.2 57.1 %copy-start.2 = (f32[256,128]{1,0:T(8,128)S(1)}, f32[256,128]{1,0:T(8,128)}, u32[]{:S(2)}) copy-start(f32[256,128]{1,0:T(8,128)} %constant.142.clone.turns) | copy-start | bytes 393220
  68.2 57.9 %copy-start.3 = (f32[8]{0:T(128)S(1)}, f32[8]{0:T(128)}, u32[]{:S(2)}) copy-start(f32[8]{0:T(128)} %skip.1) | copy-start | bytes 100
  68.2 17.5 %collective-permute-start.8 = (bf16[4,136,512]{2,1,0:T(8,128)(2,1)S(1)}, bf16[4,136,512]{2,1,0:T(8,128)(2,1)S(1)}, u32[]{:S(2)}, u32[]{:S(2)}) collective-permute-start(bf16[4,136,512]{2,1,0:T(8,128)(2,1)S(1)} %pad_maximum_fusion.refs_1_.refs_4_), channel_id=1, source_target_pairs={{0,8},{8,0},{1,9},{9,1},{2,10},{10,2},{3,11},{11,3},{4,12},{12,4},... | collective-permute-start | bytes 1671176 | tf_op jit(solution)/shard_map/ppermute | solution.py:239
  71.9 23.0 %collective-permute-start.9 = (bf16[4,136,512]{2,1,0:T(8,128)(2,1)}, bf16[4,136,512]{2,1,0:T(8,128)(2,1)S(1)}, u32[]{:S(2)}, u32[]{:S(2)}) collective-permute-start(bf16[4,136,512]{2,1,0:T(8,128)(2,1)} %collective-permute-done.7.refs_2_.refs_5_), channel_id=1, source_target_pairs={{0,8},{8,0},{1,9},{9,1},{2,10},{10,2},{3,11},{11,3},{4,12},{12,4},... | collective-permute-start | bytes 1671176 | tf_op jit(solution)/shard_map/ppermute | solution.py:239
  74.9 22.0 %collective-permute-start.10 = (bf16[4,136,512]{2,1,0:T(8,128)(2,1)S(1)}, bf16[4,136,512]{2,1,0:T(8,128)(2,1)S(1)}, u32[]{:S(2)}, u32[]{:S(2)}) collective-permute-start(bf16[4,136,512]{2,1,0:T(8,128)(2,1)S(1)} %pad_maximum_fusion.refs_1_.refs_4_), channel_id=1, source_target_pairs={{0,1},{1,0},{2,3},{3,2},{4,5},{5,4},{6,7},{7,6},{8,9},{9,8},{10,11... | collective-permute-start | bytes 1671176 | tf_op jit(solution)/shard_map/ppermute | solution.py:239
  76.8 20.1 %collective-permute-start.11 = (bf16[4,136,512]{2,1,0:T(8,128)(2,1)}, bf16[4,136,512]{2,1,0:T(8,128)(2,1)S(1)}, u32[]{:S(2)}, u32[]{:S(2)}) collective-permute-start(bf16[4,136,512]{2,1,0:T(8,128)(2,1)} %collective-permute-done.7.refs_2_.refs_5_), channel_id=1, source_target_pairs={{0,1},{1,0},{2,3},{3,2},{4,5},{5,4},{6,7},{7,6},{8,9},{9,8},{10,11... | collective-permute-start | bytes 1671176 | tf_op jit(solution)/shard_map/ppermute | solution.py:239
  85.8 11.1 %collective-permute-start.12 = (bf16[4,136,512]{2,1,0:T(8,128)(2,1)S(1)}, bf16[4,136,512]{2,1,0:T(8,128)(2,1)S(1)}, u32[]{:S(2)}, u32[]{:S(2)}) collective-permute-start(bf16[4,136,512]{2,1,0:T(8,128)(2,1)S(1)} %collective-permute-done.8.refs_3_.refs_6_), channel_id=1, source_target_pairs={{0,1},{1,0},{2,3},{3,2},{4,5},{5,4},{6,7},{7,6},{8,9},{9,8},{10,11... | collective-permute-start | bytes 1671176 | tf_op jit(solution)/shard_map/ppermute | solution.py:239
  95.0 4.0 %collective-permute-start.13 = (bf16[4,136,512]{2,1,0:T(8,128)(2,1)S(1)}, bf16[4,136,512]{2,1,0:T(8,128)(2,1)}, u32[]{:S(2)}, u32[]{:S(2)}) collective-permute-start(bf16[4,136,512]{2,1,0:T(8,128)(2,1)S(1)} %collective-permute-done.9.refs_4_.refs_7_), channel_id=1, source_target_pairs={{0,1},{1,0},{2,3},{3,2},{4,5},{5,4},{6,7},{7,6},{8,9},{9,8},{10,11... | collective-permute-start | bytes 1671176 | tf_op jit(solution)/shard_map/ppermute | solution.py:239
  104.3 21.8 %all-to-all-start.2 = ((bf16[16,4,8,128]{3,2,1,0:T(8,128)(2,1)}), bf16[16,4,8,128]{3,2,1,0:T(8,128)(2,1)S(1)}, u32[]{:S(2)}, u32[]{:S(2)}) async-start(bf16[16,4,8,128]{3,2,1,0:T(8,128)(2,1)} %shard_map.92), calls=%async_computation.2 | async-start | bytes 262144 | tf_op jit(solution)/shard_map/all_to_all | solution.py:25
  114.9 22.7 %collective-permute-start.4 = (bf16[8,2,64,128]{3,2,1,0:T(8,128)(2,1)S(1)}, bf16[8,2,64,128]{3,2,1,0:T(8,128)(2,1)S(1)}, u32[]{:S(2)}, u32[]{:S(2)}) collective-permute-start(bf16[8,2,64,128]{3,2,1,0:T(8,128)(2,1)S(1)} %slice_bitcast_fusion.refs_0_), channel_id=1, source_target_pairs={{0,64},{64,0},{128,192},{192,128},{1,65},{65,1},{129,193},{193,129... | collective-permute-start | bytes 786440 | tf_op jit(solution)/shard_map/ppermute | solution.py:239
  117.7 19.9 %collective-permute-start.5 = (bf16[8,2,64,128]{3,2,1,0:T(8,128)(2,1)S(1)}, bf16[8,2,64,128]{3,2,1,0:T(8,128)(2,1)S(1)}, u32[]{:S(2)}, u32[]{:S(2)}) collective-permute-start(bf16[8,2,64,128]{3,2,1,0:T(8,128)(2,1)S(1)} %slice_bitcast_fusion.refs_0_), channel_id=1, source_target_pairs={{0,128},{64,192},{128,0},{192,64},{1,129},{65,193},{129,1},{193,65... | collective-permute-start | bytes 786440 | tf_op jit(solution)/shard_map/ppermute | solution.py:239
  120.3 17.3 %collective-permute-start.6 = (bf16[8,2,64,128]{3,2,1,0:T(8,128)(2,1)S(1)}, bf16[8,2,64,128]{3,2,1,0:T(8,128)(2,1)}, u32[]{:S(2)}, u32[]{:S(2)}) collective-permute-start(bf16[8,2,64,128]{3,2,1,0:T(8,128)(2,1)S(1)} %slice_bitcast_fusion.refs_0_), channel_id=1, source_target_pairs={{0,192},{64,128},{128,64},{192,0},{1,193},{65,129},{129,65},{193,1... | collective-permute-start | bytes 786440 | tf_op jit(solution)/shard_map/ppermute | solution.py:239
  128.2 17.8 %all-to-all-start.3 = ((bf16[16,4,8,128]{3,2,1,0:T(8,128)(2,1)}), bf16[16,4,8,128]{3,2,1,0:T(8,128)(2,1)S(1)}, u32[]{:S(2)}, u32[]{:S(2)}) async-start(bf16[16,4,8,128]{3,2,1,0:T(8,128)(2,1)} %bitcast.11), calls=%async_computation.3 | async-start | bytes 262144 | tf_op jit(solution)/shard_map/all_to_all | solution.py:25
  (7 other events, 35.9 us)
